TPU v7x, 32 devices: a whole 2x2x4 slice. The times are simulated.
32 devices in a mesh: dp: 16 (over z, y, core), head: 2 (over x).
Axes of the slice: x: 2, y: 2, z: 4, core: 2. Of those that a mesh axis runs over, the one named last changes fastest.
Arguments:
- frames: bfloat16 [48000, 512], P(('dp', 'head')), may hold values from -6 to 6
- cotangent: bfloat16 [48000, 512], P(('dp', 'head')), may hold values from -6 to 6
- window_live: int32 [32], replicated, may hold values from 0 to 1, as said below
- language: int32 [32], replicated, may hold values from 0 to 98
- task: int32 [32], replicated, may hold values from 0 to 1
- ln1_gain: float32 [512], replicated, may hold values from 0.5 to 1.5
- ln1_offset: float32 [512], replicated, may hold values from -1.5 to 1.5
- query_weight: bfloat16 [512, 512], P('dp', 'head'), may hold values from -0.375 to 0.375
- query_bias: float32 [512], replicated, may hold values from -1.5 to 1.5
- key_weight: bfloat16 [512, 512], P('dp', 'head'), may hold values from -0.25 to 0.25
- value_weight: bfloat16 [512, 512], P('dp', 'head'), may hold values from -0.25 to 0.25
- value_bias: float32 [512], replicated, may hold values from -1.5 to 1.5
- out_weight: bfloat16 [512, 512], P('head', 'dp'), may hold values from -2.5 to 2.5
- out_bias: float32 [512], replicated, may hold values from -1.5 to 1.5
- ln2_gain: float32 [512], replicated, may hold values from 0.5 to 1.5
- ln2_offset: float32 [512], replicated, may hold values from -1.5 to 1.5
- up_weight: bfloat16 [512, 2048], P(None, ('dp', 'head')), may hold values from -0.25 to 0.25
- up_bias: float32 [2048], replicated, may hold values from -1.5 to 1.5
- down_weight: bfloat16 [2048, 512], P(('dp', 'head')), may hold values from -0.125 to 0.125
- down_bias: float32 [512], replicated, may hold values from -1.5 to 1.5
Outputs:
- output: bfloat16 [48000, 512], P(('dp', 'head'))
- grad_frames: bfloat16 [48000, 512], P(('dp', 'head'))
- grad_ln1_gain: float32 [512], replicated
- grad_ln1_offset: float32 [512], replicated
- grad_query_weight: float32 [512, 512], P('dp', 'head')
- grad_query_bias: float32 [512], replicated
- grad_key_weight: float32 [512, 512], P('dp', 'head')
- grad_value_weight: float32 [512, 512], P('dp', 'head')
- grad_value_bias: float32 [512], replicated
- grad_out_weight: float32 [512, 512], P('head', 'dp')
- grad_out_bias: float32 [512], replicated
- grad_ln2_gain: float32 [512], replicated
- grad_ln2_offset: float32 [512], replicated
- grad_up_weight: float32 [512, 2048], P(None, ('dp', 'head'))
- grad_up_bias: float32 [2048], replicated
- grad_down_weight: float32 [2048, 512], P(('dp', 'head'))
- grad_down_bias: float32 [512], replicated
Inputs may be any that keep to these rules, and one draw needn't show every extreme that they name: `window_live`: on each index of dp the first slots of its 2 hold windows (1) and the rest are empty (0); at least half of them hold windows, and some index of dp has all 2 full.
All inputs are finite; a program needn't handle non-finite values.
Results may differ from a plain program's by a relative error of at most 0.012.
The roundings to bfloat16 on the way count: a program that leaves them out, or rounds other values in their place, can miss the bound.
Values may be sent and summed in bfloat16 or wider, within the bound.
No kernel may reach another device: no remote copies, remote signals or barrier semaphores. Data moves between devices by JAX's collectives and lax.ppermute only.
A program may use at most 256 MiB of HBM per device.

v0:
```python
import functools

import jax
import jax.numpy as jnp
from jax import lax
from jax.experimental import pallas as pl
from jax.experimental.pallas import tpu as pltpu
from jax.sharding import PartitionSpec as P

FRAMES = 1500
LANGS = 99
TASKS = 2
SLOTS = 2
HEAD_DIM = 64


def layer_norm(values, gain_vec, offset_vec):
    center = jnp.mean(values, axis=-1, keepdims=True)
    centred = values - center
    spread = jnp.mean(centred * centred, axis=-1, keepdims=True)
    return centred * lax.rsqrt(spread + 1e-05) * gain_vec + offset_vec


def gelu_exact(values):
    return jax.nn.gelu(values, approximate=False)


def contract(first_mat, second_mat):
    return lax.dot_general(
        first_mat, second_mat, (((0,), (0,)), ((), ())), preferred_element_type=jnp.float32
    )


def times_t(first_mat, second_mat):
    return lax.dot_general(
        first_mat, second_mat, (((1,), (1,)), ((), ())), preferred_element_type=jnp.float32
    )


def window_weights(window_live, language, task):
    groups = language * TASKS + task
    labels = jnp.arange(LANGS * TASKS, dtype=jnp.int32)
    matches = groups[:, None] == labels[None, :]
    live_float = window_live.astype(jnp.float32)
    counts = jnp.sum(jnp.where(matches, live_float[:, None], 0.0), axis=0)
    present = jnp.sum((counts > 0.5).astype(jnp.float32))
    own_count = jnp.sum(jnp.where(matches, counts[None, :], 0.0), axis=1)
    return live_float * jnp.sum(live_float) / (present * jnp.maximum(own_count, 1.0))


def window_scores(queries, keys_all):
    return jnp.einsum("qhd,khd->hqk", queries, keys_all, preferred_element_type=jnp.float32) * 0.125


def attend_forward(record):
    queries, keys_all, values_all = record
    scores = window_scores(queries, keys_all)
    highest_score = jnp.max(scores, axis=-1, keepdims=True)
    expo = jnp.exp(scores - highest_score)
    totals = jnp.sum(expo, axis=-1, keepdims=True)
    attn_probs = (expo / totals).astype(jnp.bfloat16)
    context = jnp.einsum("hqk,khd->qhd", attn_probs, values_all, preferred_element_type=jnp.float32)
    return (context.astype(jnp.bfloat16), (highest_score + jnp.log(totals))[..., 0])


def attend_backward(record):
    queries, keys_all, values_all, log_totals, grad_context = record
    scores = window_scores(queries, keys_all)
    attn_probs = jnp.exp(scores - log_totals[..., None])
    grad_probs = jnp.einsum(
        "qhd,khd->hqk", grad_context, values_all, preferred_element_type=jnp.float32
    )
    grad_values = jnp.einsum(
        "hqk,qhd->khd",
        attn_probs.astype(jnp.bfloat16),
        grad_context,
        preferred_element_type=jnp.float32,
    )
    row_delta = jnp.sum(grad_probs * attn_probs, axis=-1, keepdims=True)
    grad_scores = (attn_probs * (grad_probs - row_delta)).astype(jnp.bfloat16)
    grad_queries = (
        jnp.einsum("hqk,khd->qhd", grad_scores, keys_all, preferred_element_type=jnp.float32)
        * 0.125
    )
    grad_keys = (
        jnp.einsum("hqk,qhd->khd", grad_scores, queries, preferred_element_type=jnp.float32) * 0.125
    )
    return (
        grad_queries.astype(jnp.bfloat16),
        grad_keys.astype(jnp.bfloat16),
        grad_values.astype(jnp.bfloat16),
    )


def on_device(
    frames,
    cotangent,
    window_live,
    language,
    task,
    ln1_gain,
    ln1_offset,
    query_weight,
    query_bias,
    key_weight,
    value_weight,
    value_bias,
    out_weight,
    out_bias,
    ln2_gain,
    ln2_offset,
    up_weight,
    up_bias,
    down_weight,
    down_bias,
):
    local_rows = frames.shape[0]
    head_index = lax.axis_index("head")
    data_index = lax.axis_index("dp")
    per_window = window_weights(window_live, language, task)
    slot_ids = (
        head_index * local_rows + jnp.arange(local_rows, dtype=jnp.int32)
    ) // FRAMES + data_index * SLOTS
    window_ids = jnp.arange(per_window.shape[0], dtype=jnp.int32)
    frame_match = slot_ids[:, None] == window_ids[None, :]
    frame_weight = jnp.sum(jnp.where(frame_match, per_window[None, :], 0.0), axis=1)
    frame_live = jnp.sum(
        jnp.where(frame_match, window_live.astype(jnp.float32)[None, :], 0.0), axis=1
    )
    inputs = frames.astype(jnp.float32)
    normed, ln1_back = jax.vjp(layer_norm, inputs, ln1_gain, ln1_offset)
    normed_low = normed.astype(jnp.bfloat16)
    query_head, key_head, value_head, out_head = (
        lax.all_gather(query_weight, "dp", axis=0, tiled=True),
        lax.all_gather(key_weight, "dp", axis=0, tiled=True),
        lax.all_gather(value_weight, "dp", axis=0, tiled=True),
        lax.all_gather(out_weight, "dp", axis=1, tiled=True),
    )
    head_width = query_head.shape[1]
    local_heads = head_width // HEAD_DIM
    joint_weight = jnp.concatenate([query_head, key_head, value_head], axis=1)
    joint_bias = jnp.concatenate(
        [
            lax.dynamic_slice_in_dim(query_bias, head_index * head_width, head_width),
            jnp.zeros((head_width,), jnp.float32),
            lax.dynamic_slice_in_dim(value_bias, head_index * head_width, head_width),
        ]
    )
    normed_all = lax.all_gather(normed_low, "head", axis=0, tiled=True)
    projected = (
        jnp.dot(normed_all, joint_weight, preferred_element_type=jnp.float32) + joint_bias
    ).astype(jnp.bfloat16)
    shaped = projected.reshape(-1, FRAMES, 3, local_heads, HEAD_DIM)
    queries = shaped[:, :, 0]
    keys_all = shaped[:, :, 1]
    values_all = shaped[:, :, 2]
    context, log_totals = lax.map(attend_forward, (queries, keys_all, values_all))
    context_flat = context.reshape(-1, head_width)
    branch = lax.psum_scatter(
        jnp.dot(context_flat, out_head, preferred_element_type=jnp.float32),
        "head",
        scatter_dimension=0,
        tiled=True,
    )
    hidden = inputs + branch + out_bias
    normed_two, ln2_back = jax.vjp(layer_norm, hidden, ln2_gain, ln2_offset)
    normed_two_low = normed_two.astype(jnp.bfloat16)
    up_full, down_full = (
        lax.all_gather(up_weight, ("dp", "head"), axis=1, tiled=True),
        lax.all_gather(down_weight, ("dp", "head"), axis=0, tiled=True),
    )
    pre_act = jnp.dot(normed_two_low, up_full, preferred_element_type=jnp.float32) + up_bias
    activated, gelu_back = jax.vjp(gelu_exact, pre_act)
    activated_low = activated.astype(jnp.bfloat16)
    result = (
        hidden + jnp.dot(activated_low, down_full, preferred_element_type=jnp.float32) + down_bias
    )
    output = (result * frame_live[:, None]).astype(jnp.bfloat16)
    grad_result = cotangent.astype(jnp.float32) * frame_weight[:, None]
    grad_two = grad_result.astype(jnp.bfloat16)
    grad_down = contract(activated_low, grad_two)
    grad_down_bias = jnp.sum(grad_two.astype(jnp.float32), axis=0)
    grad_activated = times_t(grad_two, down_full)
    grad_pre = gelu_back(grad_activated)[0].astype(jnp.bfloat16)
    grad_up = contract(normed_two_low, grad_pre)
    grad_up_bias = jnp.sum(grad_pre.astype(jnp.float32), axis=0)
    grad_normed_two = times_t(grad_pre, up_full)
    grad_hidden_ln, grad_ln2_gain, grad_ln2_offset = ln2_back(grad_normed_two)
    grad_hidden = grad_result + grad_hidden_ln
    grad_branch = grad_hidden.astype(jnp.bfloat16)
    grad_out_bias = jnp.sum(grad_branch.astype(jnp.float32), axis=0)
    branch_all = lax.all_gather(grad_branch, "head", axis=0, tiled=True)
    grad_context = times_t(branch_all, out_head).astype(jnp.bfloat16)
    grad_out_head = contract(context_flat, branch_all)
    grad_context_win = grad_context.reshape(-1, FRAMES, local_heads, HEAD_DIM)
    grad_queries, grad_keys, grad_values = lax.map(
        attend_backward, (queries, keys_all, values_all, log_totals, grad_context_win)
    )
    grad_joint = jnp.concatenate(
        [
            grad_queries.reshape(-1, head_width),
            grad_keys.reshape(-1, head_width),
            grad_values.reshape(-1, head_width),
        ],
        axis=1,
    )
    grad_joint_weight = contract(normed_all, grad_joint)
    joint_sums = jnp.sum(grad_joint.astype(jnp.float32), axis=0)
    empty_vec = jnp.zeros((query_bias.shape[0],), jnp.float32)
    grad_query_bias = lax.dynamic_update_slice(
        empty_vec, joint_sums[:head_width], (head_index * head_width,)
    )
    grad_value_bias = lax.dynamic_update_slice(
        empty_vec, joint_sums[2 * head_width :], (head_index * head_width,)
    )
    grad_normed = lax.psum_scatter(
        times_t(grad_joint, joint_weight), "head", scatter_dimension=0, tiled=True
    )
    grad_inputs_ln, grad_ln1_gain, grad_ln1_offset = ln1_back(grad_normed)
    grad_frames = (grad_hidden + grad_inputs_ln).astype(jnp.bfloat16)
    grad_query_w, grad_key_w, grad_value_w, grad_out_w = (
        lax.psum_scatter(grad_joint_weight[:, :head_width], "dp", scatter_dimension=0, tiled=True),
        lax.psum_scatter(
            grad_joint_weight[:, head_width : 2 * head_width], "dp", scatter_dimension=0, tiled=True
        ),
        lax.psum_scatter(
            grad_joint_weight[:, 2 * head_width :], "dp", scatter_dimension=0, tiled=True
        ),
        lax.psum_scatter(grad_out_head, "dp", scatter_dimension=1, tiled=True),
    )
    grad_up_w, grad_down_w = (
        lax.psum_scatter(grad_up, ("dp", "head"), scatter_dimension=1, tiled=True),
        lax.psum_scatter(grad_down, ("dp", "head"), scatter_dimension=0, tiled=True),
    )
    (
        sum_ln1_gain,
        sum_ln1_offset,
        sum_query_bias,
        sum_value_bias,
        sum_out_bias,
        sum_ln2_gain,
        sum_ln2_offset,
        sum_up_bias,
        sum_down_bias,
    ) = lax.psum(
        (
            grad_ln1_gain,
            grad_ln1_offset,
            grad_query_bias,
            grad_value_bias,
            grad_out_bias,
            grad_ln2_gain,
            grad_ln2_offset,
            grad_up_bias,
            grad_down_bias,
        ),
        ("dp", "head"),
    )
    return (
        output,
        grad_frames,
        sum_ln1_gain,
        sum_ln1_offset,
        grad_query_w,
        sum_query_bias,
        grad_key_w,
        grad_value_w,
        sum_value_bias,
        grad_out_w,
        sum_out_bias,
        sum_ln2_gain,
        sum_ln2_offset,
        grad_up_w,
        sum_up_bias,
        grad_down_w,
        sum_down_bias,
    )


LANES = 128
PADDED = 1536
LOG2E = 1.4426950408889634
MASKED = -30000.0
F32 = jnp.float32
BF16 = jnp.bfloat16
LN1_GAIN, LN1_OFFSET, OUT_BIAS, LN2_GAIN, LN2_OFFSET, DOWN_BIAS = range(6)
WEIGHT, LIVE, QUERY_BIAS, VALUE_BIAS, UP_BIAS = 6, 7, 8, 10, 11
BIT_X, BIT_CORE, BIT_Y, BIT_Z = 1, 2, 4, 8
LAYERS = 4


def dot_on(first_mat, second_mat, first_dim, second_dim):
    return lax.dot_general(
        first_mat,
        second_mat,
        (((first_dim,), (second_dim,)), ((), ())),
        preferred_element_type=F32,
    )


def params(microseconds, mebibytes):
    return dict(
        compiler_params=pltpu.CompilerParams(vmem_limit_bytes=mebibytes << 20),
        cost_estimate=pl.CostEstimate(
            flops=int(microseconds * 1e9), bytes_accessed=1 << 20, transcendentals=0
        ),
    )


def whole(shape):
    return pl.BlockSpec(shape, lambda *_: (0,) * len(shape), pipeline_mode=pl.Buffered(1))


def struct(shape, dtype):
    return jax.ShapeDtypeStruct(shape, dtype)


def place():
    dp = lax.axis_index("dp")
    return dp, lax.axis_index("head")


def pack_kernel(
    live_ref,
    language_ref,
    task_ref,
    query_ref,
    key_ref,
    value_ref,
    out_ref,
    up_ref,
    down_ref,
    upb_ref,
    qb_ref,
    vb_ref,
    *refs,
):
    vectors, (pieces_ref, big_ref, table_ref) = refs[:6], refs[6:]
    rows, half = query_ref.shape
    ff = down_ref.shape[0]
    dp, side = place()
    for j, ref in enumerate((query_ref, key_ref, value_ref)):
        pieces_ref[0, j * rows : (j + 1) * rows, :] = ref[...]
    up = up_ref[...]
    big_ref[0:ff, :] = down_ref[:, 0:half]
    big_ref[ff : 2 * ff, :] = down_ref[:, half:]
    big_ref[2 * ff : 3 * ff, :] = up[:, 0:half]
    big_ref[3 * ff : 4 * ff, :] = up[:, half:]
    big_ref[4 * ff :, :] = out_ref[...]
    for j, ref in enumerate(vectors):
        table_ref[j : j + 1, :] = ref[...]
    for j, ref in ((QUERY_BIAS, qb_ref), (VALUE_BIAS, vb_ref)):
        first, second = ref[:, 0:half], ref[:, half:]
        table_ref[j : j + 1, 0:half] = jnp.where(side == 0, second, first)
        table_ref[j : j + 1, half:] = jnp.where(side == 0, first, second)
    table_ref[QUERY_BIAS + 1 : QUERY_BIAS + 2, :] = jnp.zeros((1, 2 * half), F32)
    for j in range(4):
        table_ref[UP_BIAS + j : UP_BIAS + j + 1, :] = upb_ref[:, j * 2 * half : (j + 1) * 2 * half]
    slots = live_ref.shape[0]
    lane = lax.broadcasted_iota(jnp.int32, (1, LANES), 1)
    groups = jnp.full((1, LANES), -1, jnp.int32)
    live = jnp.zeros((1, LANES), F32)
    for t in range(slots):
        groups = jnp.where(lane == t, language_ref[t] * TASKS + task_ref[t], groups)
        live = jnp.where(lane == t, live_ref[t].astype(F32), live)
    counts = jnp.zeros((1, LANES), F32)
    for t in range(slots):
        group = language_ref[t] * TASKS + task_ref[t]
        counts = counts + jnp.where(groups == group, live_ref[t].astype(F32), 0.0)
    counts = jnp.maximum(counts, 1.0)
    shares = jnp.broadcast_to(live / counts, (8, LANES))
    present = jnp.floor(jnp.sum(shares, axis=1, keepdims=True)[0:1] + 0.5)
    total = jnp.sum(jnp.broadcast_to(live, (8, LANES)), axis=1, keepdims=True)[0:1]
    weights = live * total / (present * counts)
    mine = lane == dp * SLOTS + side
    for j, values in ((WEIGHT, weights), (LIVE, live)):
        picked = jnp.broadcast_to(jnp.where(mine, values, 0.0), (8, LANES))
        picked = jnp.sum(picked, axis=1, keepdims=True)[0:1]
        table_ref[j : j + 1, :] = jnp.broadcast_to(picked, (1, 2 * half))


def pack(live, language, task, query, key, value, out, up, down, up_bias, qb, vb, vectors):
    rows, half = query.shape
    ff, width = down.shape
    scalars = pl.BlockSpec(memory_space=pltpu.SMEM)
    row = lambda values: values.reshape(1, -1)
    rest = [query, key, value, out.T, up.T, down, row(up_bias), row(qb), row(vb)] + [
        row(v) for v in vectors
    ]
    return pl.pallas_call(
        pack_kernel,
        in_specs=[scalars] * 3 + [pl.BlockSpec(memory_space=pltpu.VMEM)] * len(rest),
        out_shape=[
            struct((1, 3 * rows, half), BF16),
            struct((4 * ff + rows, half), BF16),
            struct((16, width), F32),
        ],
        name="pack",
        **params(3, 58),
    )(live, language, task, *rest)


def real_rows(x_ref):
    row = pl.program_id(0) * x_ref.shape[0] + lax.broadcasted_iota(jnp.int32, x_ref.shape, 0)
    return row < FRAMES


def unit_rows(values):
    centred = values - jnp.mean(values, axis=1, keepdims=True)
    scale = lax.rsqrt(jnp.mean(centred * centred, axis=1, keepdims=True) + 1e-05)
    return centred * scale, scale


def unit_back(lifted, unit, scale):
    mean_one = jnp.mean(lifted, axis=1, keepdims=True)
    mean_two = jnp.mean(lifted * unit, axis=1, keepdims=True)
    return scale * (lifted - mean_one - unit * mean_two)


def norm_kernel(x_ref, table_ref, n_ref, nt_ref):
    unit, _ = unit_rows(jnp.where(real_rows(x_ref), x_ref[...].astype(F32), 0.0))
    normed = unit * table_ref[LN1_GAIN : LN1_GAIN + 1, :] + table_ref[LN1_OFFSET : LN1_OFFSET + 1, :]
    n_ref[...] = normed.astype(BF16)
    nt_ref[...] = normed.T.astype(BF16)


def first_norm(frames, table):
    width = frames.shape[1]
    tile = 512
    return pl.pallas_call(
        norm_kernel,
        grid=(PADDED // tile,),
        in_specs=[pl.BlockSpec((tile, width), lambda i: (i, 0)), whole(table.shape)],
        out_specs=[
            pl.BlockSpec((tile, width), lambda i: (i, 0)),
            pl.BlockSpec((width, tile), lambda i: (0, i)),
        ],
        out_shape=[struct((PADDED, width), BF16), struct((width, PADDED), BF16)],
        name="first_norm",
        **params(4, 14),
    )(frames, table)


def lane_masks(shape, h):
    lane = lax.broadcasted_iota(jnp.int32, shape, 1)
    return lane >= HEAD_DIM if h else lane < HEAD_DIM


def masked(values, h):
    own = lane_masks(values.shape, h)
    return jnp.where(own, values, 0.0)


def forward_kernel(side_at, n_ref, near_ref, far_ref, table_ref, *refs):
    (
        q_ref, k_ref, v_ref, p_ref, c_ref, inv_ref, row_ref, w_ref, keys_ref, vt_ref, small_ref
    ) = refs[-11:]
    pair, step = pl.program_id(0), pl.program_id(1)
    count, rows3, half = near_ref.shape
    rows = rows3 // 3

    @pl.when((pair == 0) & (step == 0))
    def _():
        dp, _ = place()
        for core, ref in enumerate((near_ref, far_ref)):
            for t in range(count):
                owner = dp ^ ((t & 1) * 8 + (t & 2) * 2 + (t & 4) // 2 + core)
                at = pl.ds(pl.multiple_of(owner * rows, rows), rows)
                for j in range(3):
                    w_ref[j, at, :] = ref[t, j * rows : (j + 1) * rows, :]

    @pl.when(step == 0)
    def _():
        columns = pl.ds(pl.multiple_of(pair * LANES, LANES), LANES)
        places = pl.ds(pl.multiple_of(pair * LANES + side_at * half, LANES), LANES)
        for j, out in enumerate((q_ref, k_ref, v_ref)):
            bias = table_ref[QUERY_BIAS + j : QUERY_BIAS + j + 1, places]
            out[...] = (dot_on(n_ref[...], w_ref[j, :, columns], 1, 0) + bias).astype(BF16)
        keys = k_ref[...].astype(F32) * (LOG2E * 0.125)
        queries = q_ref[...].astype(F32)
        high = keys.astype(BF16).astype(F32)
        flipped = v_ref[...].astype(F32).T
        shape = (vt_ref.shape[1], flipped.shape[1])
        real = lax.broadcasted_iota(jnp.int32, shape, 1) < FRAMES
        first = lax.broadcasted_iota(jnp.int32, shape, 0) == HEAD_DIM
        small = None
        for h in (0, 1):
            keys_ref[h, :, 0:LANES] = masked(high, h).astype(BF16)
            keys_ref[h, :, LANES:] = masked(keys - high, h).astype(BF16)
            mine = flipped[HEAD_DIM * h : HEAD_DIM * (h + 1), :]
            mine = jnp.concatenate([mine, mine[0 : shape[0] - HEAD_DIM]], axis=0)
            vt_ref[h] = jnp.where(real, jnp.where(first, 1.0, mine), 0.0).astype(BF16)
            norms = [
                jnp.max(jnp.sum(masked(m * m, h), axis=1, keepdims=True)) for m in (queries, keys)
            ]
            fits = (norms[0] < 1e18) & (norms[1] < 1e18) & (norms[0] * norms[1] < 50.0 * 50.0)
            small = fits if small is None else small & fits
        small_ref[0] = small.astype(jnp.int32)

    tile = c_ref.shape[0]
    tail = FRAMES // 16 * 16

    def attend(start, size, at, shift):
        queries = q_ref[pl.ds(start, size), :]
        queries = jnp.concatenate([queries, queries], axis=1)
        contexts, inverses = [], []
        for h in (0, 1):
            scores = dot_on(keys_ref[h], queries, 1, 1)
            if shift:
                real = lax.broadcasted_iota(jnp.int32, scores.shape, 0) < FRAMES
                scores = jnp.where(real, scores, -1e30)
                scores = scores - jnp.max(scores, axis=0, keepdims=True)
            probs = jnp.exp2(scores)
            low = probs.astype(BF16)
            p_ref[h, 0:tail, at] = low[0:tail]
            last = probs[tail:]
            real = lax.broadcasted_iota(jnp.int32, last.shape, 0) < FRAMES - tail
            p_ref[h, tail:, at] = jnp.where(real, last, 0.0).astype(BF16)
            summed = dot_on(vt_ref[h], low, 1, 0)
            inverse = 1.0 / summed[HEAD_DIM : HEAD_DIM + 1, :]
            row_ref[h : h + 1, at] = inverse
            contexts.append(summed[0:HEAD_DIM, :] * inverse)
            inverses.append(jnp.broadcast_to(inverse, (HEAD_DIM, inverse.shape[1])))
        return jnp.concatenate(contexts, axis=0).T.astype(BF16), jnp.concatenate(inverses, axis=0).T

    @pl.when(small_ref[0] == 1)
    def _():
        c_ref[...], inv_ref[...] = attend(step * tile, tile, slice(0, tile), False)

    @pl.when(small_ref[0] == 0)
    def _():
        size = 2 * LANES

        @pl.loop(0, tile // size)
        def _(t):
            at = pl.ds(pl.multiple_of(t * size, size), size)
            start = pl.multiple_of(step * tile + t * size, size)
            c_ref[at, :], inv_ref[at, :] = attend(start, size, at, True)


def attend_forward_fast(side_at, normed, near, far, table, before=()):
    rows, width = normed.shape
    half = near.shape[2]
    pairs = half // LANES
    tile = 768
    at = side_at * pairs
    block = pl.BlockSpec((tile, LANES), lambda p, i: (i, p + at))
    full = pl.BlockSpec((rows, LANES), lambda p, i: (0, p + at))
    weights = pl.BlockSpec((3, width, half), lambda p, i: (0, 0, side_at))
    return pl.pallas_call(
        functools.partial(forward_kernel, side_at),
        grid=(pairs, rows // tile),
        in_specs=[whole(normed.shape), whole(near.shape), whole(far.shape), whole(table.shape)]
        + [pl.BlockSpec(memory_space=pl.ANY)] * len(before),
        out_specs=[
            full, full, full,
            pl.BlockSpec((2, rows, tile), lambda p, i: (p + at, 0, i)),
            block, block,
            pl.BlockSpec((None, 8, tile), lambda p, i: (p + at, 0, i)),
            weights,
        ],
        out_shape=[struct((rows, width), BF16)] * 3
        + [
            struct((width // HEAD_DIM, rows, rows), BF16),
            struct((rows, width), BF16),
            struct((rows, width), F32),
            struct((width // LANES, 8, rows), F32),
            struct((3, width, width), BF16),
        ],
        scratch_shapes=[
            pltpu.VMEM((2, rows, 2 * LANES), BF16),
            pltpu.VMEM((2, HEAD_DIM + 16, rows), BF16),
            pltpu.SMEM((1,), jnp.int32),
        ],
        input_output_aliases={4 + j: j for j in range(len(before))},
        name="attend_forward",
        **params(15, 40),
    )(normed, near, far, table, *before)


def backward_kernel(
    first, q_ref, k_ref, v_ref, p_ref, inv_ref, row_ref, c_ref, g_ref, nt_ref, w_ref, vec_in_ref, *refs
):
    dq_ref, dk_ref, dv_ref, dw_ref, vec_ref, vals_ref, kt_ref, acck, accv, acc_one, acc_two = refs[-11:]
    pair, step = pl.program_id(0), pl.program_id(1)
    last = step == pl.num_programs(1) - 1

    @pl.when(step == 0)
    def _():
        values = v_ref[...].astype(F32)
        for h in (0, 1):
            vals_ref[h] = masked(values, h).astype(BF16)
        kt_ref[...] = k_ref[...].astype(F32).T.astype(BF16)
        acck[...] = jnp.zeros_like(acck)
        accv[...] = jnp.zeros_like(accv)

    tile = q_ref.shape[0]
    plain = q_ref[...].astype(F32)
    grads = g_ref[...].astype(F32)
    products = (grads * c_ref[...].astype(F32)).T
    divided = grads * inv_ref[...]
    diffs, queries, outers, flipped = [], [], [], []
    for h in (0, 1):
        rows = slice(HEAD_DIM * h, HEAD_DIM * (h + 1))
        row_delta = jnp.sum(products[rows], axis=0, keepdims=True)
        grad_probs = dot_on(vals_ref[h], g_ref[...], 1, 1)
        scaled = (grad_probs - row_delta) * row_ref[h : h + 1, :]
        diff = (p_ref[h].astype(F32) * scaled).astype(BF16)
        diffs.append(diff)
        outers.append(masked(divided, h).astype(BF16))
        queries.append(masked(plain, h).astype(BF16))
        flipped.append(dot_on(kt_ref[rows, :], diff, 1, 0))
    accv[...] += dot_on(p_ref[0], outers[0], 1, 0) + dot_on(p_ref[1], outers[1], 1, 0)
    acck[...] += dot_on(diffs[0], queries[0], 1, 0) + dot_on(diffs[1], queries[1], 1, 0)
    at = pl.ds(pl.multiple_of(step * tile, tile), tile)
    dq_ref[at, :] = (jnp.concatenate(flipped, axis=0) * 0.125).T.astype(BF16)

    @pl.when(last & (pair == 0))
    def _():
        acc_one[...] = jnp.zeros_like(acc_one)
        acc_two[...] = jnp.zeros_like(acc_two)
        vec_ref[...] = vec_in_ref[...]

    @pl.when(last)
    def _():
        dk_ref[...] = (acck[...] * 0.125).astype(BF16)
        dv_ref[...] = accv[...].astype(BF16)
        columns = pl.ds(pl.multiple_of((pair + first) * LANES, LANES), LANES)
        for j, ref in enumerate((dq_ref, dk_ref, dv_ref)):
            dw = dot_on(nt_ref[...], ref[...], 1, 0)
            dw_ref[j] = dw.astype(dw_ref.dtype)
            column_sums = jnp.sum(ref[...].astype(F32), axis=0, keepdims=True)
            weights = w_ref[j].astype(F32)
            acc_one[...] += weights * dw
            acc_two[...] += weights * column_sums
            if j != 1:
                vec_ref[2 + j // 2 : 3 + j // 2, columns] = column_sums

    @pl.when(last & (pair == pl.num_programs(0) - 1))
    def _():
        for j, ref in enumerate((acc_one, acc_two)):
            vec_ref[j : j + 1, :] += jnp.sum(ref[...].T, axis=0, keepdims=True)


def attend_backward_fast(
    first, pairs, q, k, v, probs, inverse, rows_inverse, context, grads, normed_t, weights, vec,
    before=(),
):
    rows, width = q.shape
    half = width // 2
    tile = 512
    block = pl.BlockSpec((tile, LANES), lambda p, i: (i, p + first))
    full = pl.BlockSpec((rows, LANES), lambda p, i: (0, p + first))
    gradient = pl.BlockSpec(
        (None, 3, width, LANES), lambda p, i: ((p + first) // 2, 0, 0, (p + first) % 2)
    )
    in_specs = [
        block, full, full,
        pl.BlockSpec((2, rows, tile), lambda p, i: (p + first, 0, i)),
        block,
        pl.BlockSpec((None, 8, tile), lambda p, i: (p + first, 0, i)),
        block, block, whole(normed_t.shape),
        pl.BlockSpec((3, width, LANES), lambda p, i: (0, 0, p + first)),
        whole(vec.shape),
    ]
    count = len(in_specs)
    return pl.pallas_call(
        functools.partial(backward_kernel, first),
        grid=(pairs, rows // tile),
        in_specs=in_specs + [pl.BlockSpec(memory_space=pl.ANY)] * len(before),
        out_specs=[full, full, full, gradient, whole(vec.shape)],
        out_shape=[struct((rows, width), BF16)] * 3
        + [struct((2, 3, width, half), BF16), struct(vec.shape, F32)],
        scratch_shapes=[
            pltpu.VMEM((2, rows, LANES), BF16),
            pltpu.VMEM((LANES, rows), BF16),
            pltpu.VMEM((rows, LANES), F32),
            pltpu.VMEM((rows, LANES), F32),
            pltpu.VMEM((width, LANES), F32),
            pltpu.VMEM((width, LANES), F32),
        ],
        input_output_aliases={count + j: j for j in range(len(before))},
        name="attend_backward",
        **params(14 * pairs, 34),
    )(q, k, v, probs, inverse, rows_inverse, context, grads, normed_t, weights, vec, *before)


def middle_kernel(masks, c_ref, x_ref, cot_ref, table_ref, *refs):
    pieces, refs = refs[: len(masks)], refs[len(masks) :]
    out_ref, g_ref, gh_ref, send_ref, keep_ref, vec_ref = refs[:6]
    up_t, up_n, down_n, down_t, out_t, upb_t, acc_up, acc_down, acc_out, acc_upb, acc_vec = refs[6:]
    step = pl.program_id(0)
    dp, side = place()
    core = lax.rem(dp, 2)
    layers, piece_rows, half = pieces[0].shape
    devices = layers * len(masks)
    width = 2 * half
    ow = width // (devices // 2)
    ff = (piece_rows - ow) // 4
    hidden_all = devices * ff
    chunk = 512
    chunks = hidden_all // chunk

    @pl.when(step == 0)
    def _():
        for mask, ref in zip(masks, pieces):
            for t in range(layers):
                owner = (dp * 2 + side) ^ (mask + (t & 1) * 2 * BIT_Z + (t & 2) // 2 * BIT_Z)
                rows = pl.ds(pl.multiple_of(owner * ff, ff), ff)
                down_n[rows, 0:half] = ref[t, 0:ff, :]
                down_n[rows, half:] = ref[t, ff : 2 * ff, :]
                up_t[rows, 0:half] = ref[t, 2 * ff : 3 * ff, :]
                up_t[rows, half:] = ref[t, 3 * ff : 4 * ff, :]
                rows = pl.ds(pl.multiple_of((owner >> 1) * ow, ow), ow)
                at = slice(0, half) if mask & BIT_X else slice(half, width)
                out_t[rows, at] = ref[t, 4 * ff :, :]
        for j in range(chunks):
            rows = slice(j * chunk, (j + 1) * chunk)
            up_n[:, rows] = up_t[rows, :].T
            down_t[:, rows] = down_n[rows, :].T
            bias = table_ref[UP_BIAS + j : UP_BIAS + j + 1, :]
            upb_t[rows, :] = jnp.broadcast_to(bias, (LANES, chunk)).T
        acc_up[...] = jnp.zeros_like(acc_up)
        acc_down[...] = jnp.zeros_like(acc_down)
        acc_out[...] = jnp.zeros_like(acc_out)
        acc_upb[...] = jnp.zeros_like(acc_upb)
        acc_vec[...] = jnp.zeros_like(acc_vec)

    def row_of(j):
        return table_ref[j : j + 1, :]

    tile = x_ref.shape[0]
    real = real_rows(x_ref)
    branch = dot_on(c_ref[...], out_t[...], 1, 1)
    hidden = jnp.where(real, x_ref[...].astype(F32), 0.0) + branch + row_of(OUT_BIAS)
    unit, scale = unit_rows(hidden)
    normed = (unit * row_of(LN2_GAIN) + row_of(LN2_OFFSET)).astype(BF16)
    grad_result = jnp.where(real, cot_ref[...].astype(F32), 0.0) * row_of(WEIGHT)
    grad_two = grad_result.astype(BF16)
    result_t = jnp.zeros((width, tile), F32)
    grad_normed_t = jnp.zeros((width, tile), F32)
    for j in range(chunks):
        rows = slice(j * chunk, (j + 1) * chunk)
        slots = slice(j * chunk // ff, (j + 1) * chunk // ff)
        pre = dot_on(up_t[rows, :], normed, 1, 1) + upb_t[rows, 0:1]
        bell = 0.5 + 0.5 * lax.erf(pre * 0.7071067811865476)
        slope = bell + pre * (jnp.exp2(pre * pre * (-0.5 * LOG2E)) * 0.3989422804014327)
        activated = (pre * bell).astype(BF16)
        result_t += dot_on(down_t[:, rows], activated, 1, 0)
        acc_down[slots] += dot_on(activated, grad_two, 1, 0).reshape(-1, ff, width)
        grad_pre = (dot_on(down_n[rows, :], grad_two, 1, 1) * slope).astype(BF16)
        rounded = grad_pre.astype(F32)
        partial = rounded[:, 0:LANES]
        for lanes in range(LANES, tile, LANES):
            partial += rounded[:, lanes : lanes + LANES]
        acc_upb[rows, :] += partial
        acc_up[slots] += dot_on(grad_pre, normed, 1, 0).reshape(-1, ff, width)
        grad_normed_t += dot_on(up_n[:, rows], grad_pre, 1, 0)
    result = hidden + result_t.T + row_of(DOWN_BIAS)
    out_ref[...] = (result * row_of(LIVE)).astype(BF16)
    grad_normed = grad_normed_t.T
    grad_hidden = grad_result + unit_back(grad_normed * row_of(LN2_GAIN), unit, scale)
    gh_ref[...] = grad_hidden
    grad_branch = grad_hidden.astype(BF16)
    g_ref[...] = dot_on(grad_branch, out_t[...], 1, 0).astype(BF16)
    acc_out[...] += dot_on(grad_hidden.T.astype(BF16), c_ref[...], 1, 0).reshape(-1, ow, width)
    for j, term in enumerate(
        (grad_branch.astype(F32), grad_normed * unit, grad_normed, grad_two.astype(F32))
    ):
        acc_vec[8 * j : 8 * j + 8, :] += jnp.sum(term.reshape(-1, 8, width), axis=0)

    @pl.when(step == pl.num_programs(0) - 1)
    def _():
        targets = devices // 2
        for ref, bit in ((keep_ref, core), (send_ref, 1 - core)):
            for t in range(targets):
                y, x, z = t // (2 * LAYERS), t // LAYERS % 2, t % LAYERS
                at = t * piece_rows
                chip = z * 2 + y
                slot = chip * 4 + bit * 2 + x
                near = pl.ds(pl.multiple_of((1 - (side ^ x)) * half, half), half)
                ref[at : at + ff, :] = acc_down[slot, :, 0:half].astype(BF16)
                ref[at + ff : at + 2 * ff, :] = acc_down[slot, :, half:].astype(BF16)
                ref[at + 2 * ff : at + 3 * ff, :] = acc_up[slot, :, 0:half].astype(BF16)
                ref[at + 3 * ff : at + 4 * ff, :] = acc_up[slot, :, half:].astype(BF16)
                ref[at + 4 * ff : at + piece_rows, :] = acc_out[chip * 2 + bit, :, near].astype(BF16)
        for j in range(4):
            total = jnp.sum(acc_vec[8 * j : 8 * j + 8, :], axis=0, keepdims=True)
            vec_ref[2 * j : 2 * j + 1, :] = total[:, 0:half]
            vec_ref[2 * j + 1 : 2 * j + 2, :] = total[:, half:]
        for j in range(chunks):
            total = jnp.sum(acc_upb[j * chunk : (j + 1) * chunk, :].T, axis=0, keepdims=True)
            for i in range(chunk // half):
                at = 8 + j * (chunk // half) + i
                vec_ref[at : at + 1, :] = total[:, i * half : (i + 1) * half]
        store_two(send_ref, targets * piece_rows, vec_ref[...])


def middle(context, frames, cotangent, table, masks, pieces):
    rows, width = context.shape
    layers, piece_rows, half = pieces[0].shape
    devices = layers * len(masks)
    tile = 512
    ow = width // (devices // 2)
    ff = (piece_rows - ow) // 4
    hidden_all = devices * ff
    body = devices // 2 * piece_rows
    wide = pl.BlockSpec((tile, width), lambda i: (i, 0))
    return pl.pallas_call(
        functools.partial(middle_kernel, masks),
        grid=(rows // tile,),
        in_specs=[wide, wide, wide, whole(table.shape)] + [whole(p.shape) for p in pieces],
        out_specs=[wide, wide, wide, whole((body + 32, half)), whole((body, half)), whole((16, half))],
        out_shape=[
            struct(frames.shape, BF16),
            struct((rows, width), BF16),
            struct((rows, width), F32),
            struct((body + 32, half), BF16),
            struct((body, half), BF16),
            struct((16, half), F32),
        ],
        scratch_shapes=[
            pltpu.VMEM((hidden_all, width), BF16),
            pltpu.VMEM((width, hidden_all), BF16),
            pltpu.VMEM((hidden_all, width), BF16),
            pltpu.VMEM((width, hidden_all), BF16),
            pltpu.VMEM((width, width), BF16),
            pltpu.VMEM((hidden_all, LANES), F32),
            pltpu.VMEM((devices, ff, width), F32),
            pltpu.VMEM((devices, ff, width), F32),
            pltpu.VMEM((width // ow, ow, width), F32),
            pltpu.VMEM((hidden_all, LANES), F32),
            pltpu.VMEM((32, width), F32),
        ],
        name="middle",
        **params(38, 48),
    )(context, frames, cotangent, table, *pieces)


def store_two(ref, at, values):
    count = values.shape[0]
    high = values.astype(BF16)
    ref[at : at + count, :] = high
    ref[at + count : at + 2 * count, :] = (values - high.astype(F32)).astype(BF16)


def load_two(ref, at, count):
    return ref[at : at + count, :].astype(F32) + ref[at + count : at + 2 * count, :].astype(F32)


def spread_kernel(count, masks, keep_ref, vec_ref, *refs):
    came, (mine_ref, sum_ref, *sends) = refs[:count], refs[count:]
    size, half = mine_ref.shape
    dp, side = place()
    parts = keep_ref.shape[0] // size
    vec_rows = vec_ref.shape[0]
    vec = vec_ref[...]
    for ref in came:
        vec += load_two(ref, ref.shape[0] - 2 * vec_rows, vec_rows)
    sum_ref[...] = vec

    def total(part):
        rows = pl.ds(pl.multiple_of(part * size, 32), size)
        values = keep_ref[rows, :].astype(F32)
        for ref in came:
            if ref.shape[0] > 2 * vec_rows:
                values += ref[rows, :].astype(F32)
        return values

    own = masks[0](dp, side)
    mine_ref[...] = total(own)
    for mask, ref in zip(masks[1:], sends):
        if mask is not None:
            ref[0:size, :] = total(own ^ mask).astype(BF16)
        store_two(ref, ref.shape[0] - 2 * vec_rows, vec)


def spread(keep, vec, came, own_part, masks, parts):
    rows, half = keep.shape
    size = rows // parts
    tail = 2 * vec.shape[0]
    vmem = pl.BlockSpec(memory_space=pltpu.VMEM)
    return pl.pallas_call(
        functools.partial(spread_kernel, len(came), (own_part, *masks)),
        in_specs=[vmem] * (2 + len(came)),
        out_specs=[vmem] * (2 + len(masks)),
        out_shape=[struct((size, half), F32), struct(vec.shape, F32)]
        + [struct(((0 if m is None else size) + tail, half), BF16) for m in masks],
        name="spread",
        **params(3, 14),
    )(keep, vec, *came)


def swap(values, mask):
    devices = lax.axis_size("dp") * lax.axis_size("head")
    return lax.ppermute(values, ("dp", "head"), [(i, i ^ mask) for i in range(devices)])


def part_xy(dp, side):
    return ((dp >> 1) & 1) * 2 + side


def part_y(dp, side):
    return (dp >> 1) & 1


def part_z(dp, side):
    return dp >> 2


def gather_kernel(table_ref, dw_ref, got_ref, vec_in_ref, send_ref, keep_ref, vec_ref, vsend_ref):
    dp, side = place()
    core = lax.rem(dp, 2)
    width = table_ref.shape[1]
    half = width // 2
    ow = width // 16
    for ref, bit in ((keep_ref, core), (send_ref, 1 - core)):
        for t in range(2 * LAYERS):
            chip = t % LAYERS * 2 + t // LAYERS
            rows = pl.ds(pl.multiple_of((chip * 2 + bit) * ow, ow), ow)
            for j in range(3):
                at = t * 3 * ow + j * ow
                both = dw_ref[j, rows, :].astype(F32) + got_ref[j, rows, :].astype(F32)
                ref[at : at + ow, :] = both.astype(ref.dtype)
    one, two = vec_in_ref[0:1, :], vec_in_ref[1:2, :]
    gain = table_ref[LN1_GAIN : LN1_GAIN + 1, :]
    offset = table_ref[LN1_OFFSET : LN1_OFFSET + 1, :]
    grad_gain = (one - offset * two) / gain
    for j, values in ((0, grad_gain), (2, two)):
        vec_ref[j : j + 1, :] = values[:, 0:half]
        vec_ref[j + 1 : j + 2, :] = values[:, half:]
    for j in (0, 1):
        other, own = vec_in_ref[2 + j : 3 + j, 0:half], vec_in_ref[2 + j : 3 + j, half:]
        vec_ref[4 + 2 * j : 5 + 2 * j, :] = jnp.where(side == 0, own, other)
        vec_ref[5 + 2 * j : 6 + 2 * j, :] = jnp.where(side == 0, other, own)
    store_two(send_ref, 24 * ow, vec_ref[...])
    store_two(vsend_ref, 0, vec_ref[...])


def gather_grads(table, dw, got, vec):
    width = table.shape[1]
    half = width // 2
    rows = 24 * (width // 16)
    shapes = [((rows + 16, half), BF16), ((rows, half), F32), ((8, half), F32), ((16, half), BF16)]
    return pl.pallas_call(
        gather_kernel,
        grid=(1,),
        in_specs=[
            whole(table.shape),
            pl.BlockSpec((None, 3, width, half), lambda i: (1, 0, 0, 0)),
            whole(got.shape),
            whole(vec.shape),
        ],
        out_specs=[whole(shape) for shape, _ in shapes],
        out_shape=[struct(*shape) for shape in shapes],
        name="gather_grads",
        **params(2, 12),
    )(table, dw, got, vec)


def finish_kernel(ff, ow, mine_ref, vec_ref, mine_w_ref, vec_w_ref, *refs):
    came, came_w, outs = refs[: LAYERS - 1], refs[LAYERS - 1 : 2 * LAYERS - 2], refs[2 * LAYERS - 2 :]
    down_ref, up_ref, out_ref, *outs = outs

    def total(mine, vec, parts):
        size = mine.shape[0]
        values, sums = mine[...], vec[...]
        for ref in parts:
            values += ref[0:size, :].astype(F32)
            sums += load_two(ref, size, vec.shape[0])
        return values, sums

    half = mine_ref.shape[1]
    values, vec = total(mine_ref, vec_ref, came)
    down_ref[:, 0:half] = values[0:ff]
    down_ref[:, half:] = values[ff : 2 * ff]
    up_ref[:, 0:half] = values[2 * ff : 3 * ff]
    up_ref[:, half:] = values[3 * ff : 4 * ff]
    out_ref[...] = values[4 * ff :]
    values, vec_w = total(mine_w_ref, vec_w_ref, came_w)
    for j in range(3):
        outs[j][...] = values[j * ow : (j + 1) * ow]
    at = 0
    rows = [vec[j : j + 1] for j in range(vec.shape[0])] + [
        vec_w[j : j + 1] for j in range(vec_w.shape[0])
    ]
    for ref in outs[3:]:
        for j in range(ref.shape[1] // half):
            ref[:, j * half : (j + 1) * half] = rows[at]
            at += 1


def finish(mine, vec, mine_w, vec_w, came, came_w, ff, ow):
    half = mine.shape[1]
    vmem = pl.BlockSpec(memory_space=pltpu.VMEM)
    shapes = [(ff, 2 * half), (ff, 2 * half), (ow, half)] + [(ow, half)] * 3
    shapes += [(1, 2 * half)] * 4 + [(1, 8 * half)] + [(1, 2 * half)] * 4
    return pl.pallas_call(
        functools.partial(finish_kernel, ff, ow),
        in_specs=[vmem] * (4 + len(came) + len(came_w)),
        out_specs=[vmem] * len(shapes),
        out_shape=[struct(shape, F32) for shape in shapes],
        name="finish",
        **params(3, 12),
    )(mine, vec, mine_w, vec_w, *came, *came_w)


def input_grad_kernel(x_ref, gh_ref, table_ref, w_ref, dq_ref, dk_ref, dv_ref, gf_ref):
    total = dot_on(dq_ref[...], w_ref[0], 1, 1)
    total += dot_on(dk_ref[...], w_ref[1], 1, 1)
    total += dot_on(dv_ref[...], w_ref[2], 1, 1)
    unit, scale = unit_rows(jnp.where(real_rows(x_ref), x_ref[...].astype(F32), 0.0))
    lifted = total * table_ref[LN1_GAIN : LN1_GAIN + 1, :]
    gf_ref[...] = (gh_ref[...] + unit_back(lifted, unit, scale)).astype(BF16)


def input_grads(frames, grad_hidden, table, weights, grads):
    rows, width = grad_hidden.shape
    tile = 512
    wide = pl.BlockSpec((tile, width), lambda i: (i, 0))
    return pl.pallas_call(
        input_grad_kernel,
        grid=(rows // tile,),
        in_specs=[wide, wide, whole(table.shape), whole(weights.shape), wide, wide, wide],
        out_specs=wide,
        out_shape=struct(frames.shape, BF16),
        name="input_grads",
        **params(9, 20),
    )(frames, grad_hidden, table, weights, *grads)


def on_whole_windows(
    frames,
    cotangent,
    window_live,
    language,
    task,
    ln1_gain,
    ln1_offset,
    query_weight,
    query_bias,
    key_weight,
    value_weight,
    value_bias,
    out_weight,
    out_bias,
    ln2_gain,
    ln2_offset,
    up_weight,
    up_bias,
    down_weight,
    down_bias,
):
    ow, ff = query_weight.shape[0], up_weight.shape[1]
    pieces, big, table = pack(
        window_live,
        language,
        task,
        query_weight,
        key_weight,
        value_weight,
        out_weight,
        up_weight,
        down_weight,
        up_bias,
        query_bias,
        value_bias,
        [ln1_gain, ln1_offset, out_bias, ln2_gain, ln2_offset, down_bias],
    )
    together = lax.optimization_barrier

    def doubled(values, came):
        return jnp.concatenate([values, came], axis=0)

    came = swap(pieces, 2 * BIT_Z)
    normed, normed_t = first_norm(frames, table)
    came, normed, big = together((came, normed, big[None]))
    pieces = doubled(pieces, came)
    came, came_big = together((swap(pieces, BIT_Z), swap(big, 2 * BIT_Z)))
    pieces, big = doubled(pieces, came), doubled(big, came_big)
    came, came_big = together((swap(pieces, BIT_Y), swap(big, BIT_Z)))
    near, big = doubled(pieces, came), doubled(big, came_big)
    far = swap(near, BIT_CORE)
    near_other = swap(near, BIT_X)

    normed_one, big, far = together((normed, big, far))
    big_y = swap(big, BIT_Y)
    big_x = swap(big, BIT_X)
    half_done = list(attend_forward_fast(1, normed_one, near, far, table))
    near_other, big_y, big_x, half_done[4] = together((near_other, big_y, big_x, half_done[4]))
    far_other = swap(near_other, BIT_CORE)
    big_xy = swap(big_y, BIT_X)
    across = [swap(p, BIT_CORE) for p in (big, big_y, big_x)]
    q, k, v, probs, context, inverse, rows_inverse, weights = attend_forward_fast(
        0, normed, near_other, far_other, table, half_done
    )
    big_xy, context = together((big_xy, context))
    across.append(swap(big_xy, BIT_CORE))
    masks = (0, BIT_Y, BIT_X, BIT_X | BIT_Y)
    masks += tuple(m | BIT_CORE for m in masks)
    output, grads, grad_hidden, send, keep, vec = middle(
        context, frames, cotangent, table, masks, [big, big_y, big_x, big_xy, *across]
    )

    def backward(first, pairs, grads, vec, before=()):
        return attend_backward_fast(
            first, pairs, q, k, v, probs, inverse, rows_inverse, context, grads, normed_t, weights,
            vec, before,
        )

    came = swap(send, BIT_CORE)
    *done, vec_w = backward(0, 1, grads, jnp.zeros_like(table[0:8]))
    came, grads = lax.optimization_barrier((came, grads))
    mine, vec, *sends = spread(keep, vec, [came], part_xy, (1, 2, 3), 4)
    *sends, grads = lax.optimization_barrier((*sends, grads))
    came_xy = [swap(s, m) for s, m in zip(sends, (BIT_X, BIT_Y, BIT_X | BIT_Y))]
    *done, vec_w = backward(1, 2, grads, vec_w, done)
    across = done[3][0]
    came_xy, grads, across = lax.optimization_barrier((came_xy, grads, across))
    mine, vec, *sends = spread(mine, vec, came_xy, part_z, (1, 2, 3), LAYERS)
    *sends, grads, across = lax.optimization_barrier((*sends, grads, across))
    got = swap(across, BIT_X)
    came_z = [swap(s, m * BIT_Z) for s, m in zip(sends, (1, 2, 3))]
    *done, dw, vec_w = backward(3, 1, grads, vec_w, done)

    came_z, vec_w = lax.optimization_barrier((came_z, vec_w))
    send, keep_w, vec_w, vec_send = gather_grads(table, dw, got, vec_w)
    came = [swap(send, BIT_CORE), swap(vec_send, BIT_X), swap(vec_send, BIT_X | BIT_CORE)]
    mine_w, vec_w, send = spread(keep_w, vec_w, came, part_y, (1,), 2)
    came = [swap(send, BIT_Y)]
    grad_frames = input_grads(frames, grad_hidden, table, weights, done)
    came, grad_frames = lax.optimization_barrier((came, grad_frames))
    mine_w, vec_w, *sends = spread(mine_w, vec_w, came, part_z, (1, 2, 3), LAYERS)
    came_w = [swap(s, m * BIT_Z) for s, m in zip(sends, (1, 2, 3))]
    down_grad, up_grad, out_grad, query_grad, key_grad, value_grad, *vectors = finish(
        mine, vec, mine_w, vec_w, came_z, came_w, ff, ow
    )
    vectors = [v.reshape(-1) for v in vectors]
    out_bias_grad, gain_two, offset_two, down_bias_grad, up_bias_grad = vectors[:5]
    gain_one, offset_one, query_bias_grad, value_bias_grad = vectors[5:]
    return (
        output,
        grad_frames,
        gain_one,
        offset_one,
        query_grad,
        query_bias_grad,
        key_grad,
        value_grad,
        value_bias_grad,
        out_grad.T,
        out_bias_grad,
        gain_two,
        offset_two,
        up_grad.T,
        up_bias_grad,
        down_grad,
        down_bias_grad,
    )


def solution(mesh):
    placed = (
        P(("dp", "head"), None),
        P(("dp", "head"), None),
        P(),
        P(),
        P(),
        P(),
        P(),
        P("dp", "head"),
        P(),
        P("dp", "head"),
        P("dp", "head"),
        P(),
        P("head", "dp"),
        P(),
        P(),
        P(),
        P(None, ("dp", "head")),
        P(),
        P(("dp", "head"), None),
        P(),
    )
    step = on_device
    if mesh.shape["dp"] == 4 * LAYERS and mesh.shape["head"] == SLOTS:
        step = on_whole_windows
    return jax.shard_map(
        step,
        mesh=mesh,
        in_specs=placed,
        out_specs=(
            P(("dp", "head"), None),
            P(("dp", "head"), None),
            P(),
            P(),
            P("dp", "head"),
            P(),
            P("dp", "head"),
            P("dp", "head"),
            P(),
            P("head", "dp"),
            P(),
            P(),
            P(),
            P(None, ("dp", "head")),
            P(),
            P(("dp", "head"), None),
            P(),
        ),
        check_vma=False,
    )
```

profile of v0, /device:TPU:0, one launch (start us, length us, event | category | flops | bytes accessed | tf_op | source)
XLA Modules:
  0.0 227.2 jit_solution(3287373847930519529)
XLA Ops:
  0.7 2.0 pack.1
  2.7 4.0 %collective-permute-start = (bf16[1,96,256]{2,1,0:T(8,128)(2,1)}, bf16[1,96,256]{2,1,0:T(8,128)(2,1)S(1)}, u32[]{:S(2)}, u32[]{:S(2)}) collective-permute-start(bf16[1,96,256]{2,1,0:T(8,128)(2,1)} %get-tuple-element.134), channel_id=1, source_target_pairs={{0,16},{1,17},{2,18},{3,19},{4,20},{5,21},{6,22},{7,23},{8,24},{9,... | collective-permute-start | bytes 147464 | tf_op jit(solution)/shard_map/ppermute | solution.py:896
  6.7 0.8 copy-done.9
  7.5 1.7 first_norm.1
  9.1 0.4 collective-permute-done
  9.5 2.4 %collective-permute-start.2 = (bf16[1,288,256]{2,1,0:T(8,128)(2,1)S(1)}, bf16[1,288,256]{2,1,0:T(8,128)(2,1)S(1)}, u32[]{:S(2)}, u32[]{:S(2)}) collective-permute-start(bf16[1,288,256]{2,1,0:T(8,128)(2,1)S(1)} %bitcast.25), channel_id=1, source_target_pairs={{0,16},{1,17},{2,18},{3,19},{4,20},{5,21},{6,22},{7,23},{8,24},{9,... | collective-permute-start | bytes 442376 | tf_op jit(solution)/shard_map/ppermute | solution.py:896
  12.0 2.0 collective-permute-start.1
  14.0 3.4 %collective-permute-done.1 = bf16[2,96,256]{2,1,0:T(8,128)(2,1)S(1)} collective-permute-done((bf16[2,96,256]{2,1,0:T(8,128)(2,1)S(1)}, bf16[2,96,256]{2,1,0:T(8,128)(2,1)S(1)}, u32[]{:S(2)}, u32[]{:S(2)}) %collective-permute-start.1) | collective-permute-done | bytes 98336 | tf_op jit(solution)/shard_map/ppermute | solution.py:896
  17.4 1.2 collective-permute-done.2
  18.6 0.1 collective-permute-start.4
  18.8 1.6 collective-permute-start.3
  20.4 4.1 %collective-permute-done.3 = bf16[4,96,256]{2,1,0:T(8,128)(2,1)S(1)} collective-permute-done((bf16[4,96,256]{2,1,0:T(8,128)(2,1)S(1)}, bf16[4,96,256]{2,1,0:T(8,128)(2,1)S(1)}, u32[]{:S(2)}, u32[]{:S(2)}) %collective-permute-start.3) | collective-permute-done | bytes 196640 | tf_op jit(solution)/shard_map/ppermute | solution.py:896
  24.5 1.3 collective-permute-done.4
  26.0 1.6 collective-permute-start.5
  27.6 0.1 collective-permute-done.6.far_ref
  27.7 1.5 collective-permute-start.7
  29.2 1.5 collective-permute-start.8
  30.7 16.3 %attend_forward.2 = (bf16[1536,512]{1,0:T(8,128)(2,1)S(1)}, bf16[1536,512]{1,0:T(8,128)(2,1)S(1)}, bf16[1536,512]{1,0:T(8,128)(2,1)S(1)}, bf16[8,1536,1536]{2,1,...) custom-call(bf16[1536,512]{1,0:T(8,128)(2,1)S(1)} %get-tuple-element, ...), custom_call_target="tpu_custom_call" | custom-call | flops 15000000512 | bytes 1048576 | tf_op jit(solution)/shard_map/attend_forward/pallas_call | solution.py:550
  47.0 3.2 %collective-permute-done.8.refs_2_ = bf16[4,288,256]{2,1,0:T(8,128)(2,1)S(1)} collective-permute-done((bf16[4,288,256]{2,1,0:T(8,128)(2,1)S(1)}, bf16[4,288,256]{2,1,0:T(8,128)(2,1)S(1)}, u32[]{:S(2)}, u32[]{:S(2)}) %collective-permute-start.8) | collective-permute-done | bytes 589856 | tf_op jit(solution)/shard_map/ppermute | solution.py:896
  50.1 5.0 %collective-permute-start.10 = (bf16[8,96,256]{2,1,0:T(8,128)(2,1)S(1)}, bf16[8,96,256]{2,1,0:T(8,128)(2,1)S(1)}, u32[]{:S(2)}, u32[]{:S(2)}) collective-permute-start(bf16[8,96,256]{2,1,0:T(8,128)(2,1)S(1)} %collective-permute-done.5.near_ref), channel_id=1, source_target_pairs={{0,2},{1,3},{2,0},{3,1},{4,6},{5,7},{6,4},{7,5},{8,10},{9,11},{10,... | collective-permute-start | bytes 1179656 | tf_op jit(solution)/shard_map/ppermute | solution.py:896
  55.1 0.1 collective-permute-start.11
  55.2 0.4 collective-permute-start.12
  55.7 0.1 collective-permute-start.13
  55.7 0.8 collective-permute-done.10.far_ref
  56.5 16.7 %attend_forward.3 = (bf16[1536,512]{1,0:T(8,128)(2,1)S(1)}, bf16[1536,512]{1,0:T(8,128)(2,1)S(1)}, bf16[1536,512]{1,0:T(8,128)(2,1)S(1)}, bf16[8,1536,1536]{2,1,...) custom-call(bf16[1536,512]{1,0:T(8,128)(2,1)S(1)} %get-tuple-element, ...), custom_call_target="tpu_custom_call", output_to_operand_aliasing={{0}: (4, {}), {1}: (5, {}), {2}: (6, {}), {3}: (7, {}), {4}... | custom-call | flops 15000000512 | bytes 1048576 | tf_op jit(solution)/shard_map/attend_forward/pallas_call | solution.py:550
  73.2 1.2 copy-done.1
  74.3 1.1 copy-done.3
  75.5 0.4 collective-permute-start.14
  75.9 1.6 collective-permute-done.14.refs_7_
  77.5 35.9 %middle.1 = (bf16[1500,512]{1,0:T(8,128)(2,1)}, bf16[1536,512]{1,0:T(8,128)(2,1)}, f32[1536,512]{1,0:T(8,128)}, bf16[4640,256]{1,0:T(8,128)(2,1)}, bf16[4608,256]{1,0:T(8,128)(2,1)}, /*index=5*/f32[16,256]{1,0:T(8,128)S(1)}) custom-call(bf16[1536,512]{1,0:T(8,128)(2,1)} %copy-done.1, bf16[1500,512]{1,0:T(8,128)(2,1)} %x_ref.5, bf16[1500,512]{1,0:T(8,128)(2,1)} %cot_ref.1, ...), custom_call_target="tpu_custom_call" | custom-call | flops 38000001024 | bytes 1048576 | tf_op jit(solution)/shard_map/middle/pallas_call | solution.py:809
  113.4 0.4 collective-permute-start.15
  113.8 1.4 copy-done
  115.2 1.4 copy-done.2
  116.6 1.4 copy-done.4
  118.0 15.1 %attend_backward.3 = (bf16[1536,512]{1,0:T(8,128)(2,1)S(1)}, bf16[1536,512]{1,0:T(8,128)(2,1)S(1)}, bf16[1536,512]{1,0:T(8,128)(2,1)S(1)}, bf16[2,3,512,256]{3,2,1,0:T(8,128)(2,1)S(1)}, f32[8,512]{1,0:T(8,128)S(1)}) custom-call(bf16[1536,512]{1,0:T(8,128)(2,1)S(1)} %get-tuple-element.164.q_ref, bf16[1536,512]{1,0:T(8,128)(2,1)S(1)} %get-tuple-element.165.k_ref, ...), custom_call_target="tpu_custom_call" | custom-call | flops 14000000000 | bytes 1048576 | tf_op jit(solution)/shard_map/attend_backward/pallas_call | solution.py:667
  133.2 0.5 spread.4
  133.7 9.7 %collective-permute-start.16 = (bf16[1184,256]{1,0:T(8,128)(2,1)S(1)}, bf16[1184,256]{1,0:T(8,128)(2,1)S(1)}, u32[]{:S(2)}, u32[]{:S(2)}) collective-permute-start(bf16[1184,256]{1,0:T(8,128)(2,1)S(1)} %get-tuple-element.181), channel_id=1, source_target_pairs={{0,1},{1,0},{2,3},{3,2},{4,5},{5,4},{6,7},{7,6},{8,9},{9,8},{10,11... | collective-permute-start | bytes 1818632 | tf_op jit(solution)/shard_map/ppermute | solution.py:896
  143.4 1.4 collective-permute-start.17
  144.7 0.2 collective-permute-start.18
  144.9 28.5 %attend_backward.4 = (bf16[1536,512]{1,0:T(8,128)(2,1)S(1)}, bf16[1536,512]{1,0:T(8,128)(2,1)S(1)}, bf16[1536,512]{1,0:T(8,128)(2,1)S(1)}, bf16[2,3,512,256]{3,2,1,0:T(8,128)(2,1)S(1)}, f32[8,512]{1,0:T(8,128)S(1)}) custom-call(bf16[1536,512]{1,0:T(8,128)(2,1)S(1)} %get-tuple-element.164., ...), custom_call_target="tpu_custom_call", output_to_operand_aliasing={{0}: (11, {}), {1}: (12, {}), {2}: (13, {}), {3}: (14, {})} | custom-call | flops 28000000000 | bytes 1048576 | tf_op jit(solution)/shard_map/attend_backward/pallas_call | solution.py:667
  173.5 0.3 spread.5
  173.8 0.7 collective-permute-start.20
  174.5 10.3 %collective-permute-start.21 = (bf16[320,256]{1,0:T(8,128)(2,1)S(1)}, bf16[320,256]{1,0:T(8,128)(2,1)S(1)}, u32[]{:S(2)}, u32[]{:S(2)}) collective-permute-start(bf16[320,256]{1,0:T(8,128)(2,1)S(1)} %get-tuple-element.209), channel_id=1, source_target_pairs={{0,16},{1,17},{2,18},{3,19},{4,20},{5,21},{6,22},{7,23},{8,24},{9,... | collective-permute-start | bytes 491528 | tf_op jit(solution)/shard_map/ppermute | solution.py:896
  184.8 1.4 collective-permute-start.22
  186.1 1.5 collective-permute-start.19
  187.6 14.8 %attend_backward.5 = (bf16[1536,512]{1,0:T(8,128)(2,1)S(1)}, bf16[1536,512]{1,0:T(8,128)(2,1)S(1)}, bf16[1536,512]{1,0:T(8,128)(2,1)S(1)}, bf16[2,3,512,256]{3,2,1,0:T(8,128)(2,1)S(1)}, f32[8,512]{1,0:T(8,128)S(1)}) custom-call(bf16[1536,512]{1,0:T(8,128)(2,1)S(1)} %get-tuple-element.164., ...), custom_call_target="tpu_custom_call", output_to_operand_aliasing={{0}: (11, {}), {1}: (12, {}), {2}: (13, {}), {3}: (14, {})} | custom-call | flops 14000000000 | bytes 1048576 | tf_op jit(solution)/shard_map/attend_backward/pallas_call | solution.py:667
  202.4 2.4 %collective-permute-done.19.got_ref = bf16[3,512,256]{2,1,0:T(8,128)(2,1)S(1)} collective-permute-done((bf16[3,512,256]{2,1,0:T(8,128)(2,1)S(1)}, bf16[3,512,256]{2,1,0:T(8,128)(2,1)S(1)}, u32[]{:S(2)}, u32[]{:S(2)}) %collective-permute-start.19) | collective-permute-done | bytes 786464 | tf_op jit(solution)/shard_map/ppermute | solution.py:896
  204.8 0.2 gather_grads.1
  205.1 1.5 collective-permute-start.24
  206.6 0.3 collective-permute-start.25
  206.9 1.9 collective-permute-done.24.refs_1_
  208.8 0.9 collective-permute-done.25.refs_2_
  209.7 0.1 spread.6
  209.8 1.8 collective-permute-start.26
  211.6 0.4 copy-done.8
  212.1 4.7 %input_grads.1 = bf16[1500,512]{1,0:T(8,128)(2,1)} custom-call(bf16[1500,512]{1,0:T(8,128)(2,1)S(1)} %copy-done.6, f32[1536,512]{1,0:T(8,128)S(1)} %copy-done.8, f32[16,512]{1,0:T(8,128)S(1)} %copy-done.10, bf16[3,512,512]{2,1,0:T(8,128)(2,1)S(1)} %copy-done.4, bf16[1536,512]{1,0:T(8,128)(2,1)S(1)} %get-tuple-element.219.dq_ref, ...), custom_call_target="tpu_custom_call" | custom-call | flops 8999999488 | bytes 1048576 | tf_op jit(solution)/shard_map/input_grads/pallas_call | solution.py:1021
  216.7 0.3 collective-permute-done.26.refs_0_
  217.1 0.6 collective-permute-start.27
  217.7 2.4 %collective-permute-start.28 = (bf16[112,256]{1,0:T(8,128)(2,1)S(1)}, bf16[112,256]{1,0:T(8,128)(2,1)S(1)}, u32[]{:S(2)}, u32[]{:S(2)}) collective-permute-start(bf16[112,256]{1,0:T(8,128)(2,1)S(1)} %get-tuple-element.234), channel_id=1, source_target_pairs={{0,16},{1,17},{2,18},{3,19},{4,20},{5,21},{6,22},{7,23},{8,24},{9,... | collective-permute-start | bytes 172040 | tf_op jit(solution)/shard_map/ppermute | solution.py:896
  220.2 1.4 collective-permute-start.29
  221.5 0.4 collective-permute-done.27.refs_3_
  221.9 2.9 %collective-permute-done.28.refs_4_ = bf16[112,256]{1,0:T(8,128)(2,1)S(1)} collective-permute-done((bf16[112,256]{1,0:T(8,128)(2,1)S(1)}, bf16[112,256]{1,0:T(8,128)(2,1)S(1)}, u32[]{:S(2)}, u32[]{:S(2)}) %collective-permute-start.28) | collective-permute-done | bytes 57376 | tf_op jit(solution)/shard_map/ppermute | solution.py:896
  224.9 1.3 collective-permute-done.29.refs_5_
  226.1 0.8 finish.1
  (47 shorter events, 0.5 us)
Async XLA Ops:
  0.7 6.0 %copy-start.5 = (bf16[1500,512]{1,0:T(8,128)(2,1)S(1)}, bf16[1500,512]{1,0:T(8,128)(2,1)}, u32[]{:S(2)}) copy-start(bf16[1500,512]{1,0:T(8,128)(2,1)} %x_ref.5) | copy-start | bytes 4608004
  2.7 6.8 %collective-permute-start = (bf16[1,96,256]{2,1,0:T(8,128)(2,1)}, bf16[1,96,256]{2,1,0:T(8,128)(2,1)S(1)}, u32[]{:S(2)}, u32[]{:S(2)}) collective-permute-start(bf16[1,96,256]{2,1,0:T(8,128)(2,1)} %get-tuple-element.134), channel_id=1, source_target_pairs={{0,16},{1,17},{2,18},{3,19},{4,20},{5,21},{6,22},{7,23},{8,24},{9,... | collective-permute-start | bytes 147464 | tf_op jit(solution)/shard_map/ppermute | solution.py:896
  6.7 0.8 copy-start.9
  7.5 2.0 copy-start.11
  7.5 4.5 %copy-start.12 = (bf16[1,96,256]{2,1,0:T(8,128)(2,1)S(1)}, bf16[1,96,256]{2,1,0:T(8,128)(2,1)}, u32[]{:S(2)}) copy-start(bf16[1,96,256]{2,1,0:T(8,128)(2,1)} %get-tuple-element.134) | copy-start | bytes 147460
  9.5 9.1 %collective-permute-start.2 = (bf16[1,288,256]{2,1,0:T(8,128)(2,1)S(1)}, bf16[1,288,256]{2,1,0:T(8,128)(2,1)S(1)}, u32[]{:S(2)}, u32[]{:S(2)}) collective-permute-start(bf16[1,288,256]{2,1,0:T(8,128)(2,1)S(1)} %bitcast.25), channel_id=1, source_target_pairs={{0,16},{1,17},{2,18},{3,19},{4,20},{5,21},{6,22},{7,23},{8,24},{9,... | collective-permute-start | bytes 442376 | tf_op jit(solution)/shard_map/ppermute | solution.py:896
  12.0 5.4 %collective-permute-start.1 = (bf16[2,96,256]{2,1,0:T(8,128)(2,1)S(1)}, bf16[2,96,256]{2,1,0:T(8,128)(2,1)S(1)}, u32[]{:S(2)}, u32[]{:S(2)}) collective-permute-start(bf16[2,96,256]{2,1,0:T(8,128)(2,1)S(1)} %pad_maximum_fusion.3), channel_id=1, source_target_pairs={{0,8},{1,9},{2,10},{3,11},{4,12},{5,13},{6,14},{7,15},{8,0},{9,1},... | collective-permute-start | bytes 294920 | tf_op jit(solution)/shard_map/ppermute | solution.py:896
  18.6 7.2 %collective-permute-start.4 = (bf16[2,288,256]{2,1,0:T(8,128)(2,1)S(1)}, bf16[2,288,256]{2,1,0:T(8,128)(2,1)S(1)}, u32[]{:S(2)}, u32[]{:S(2)}) collective-permute-start(bf16[2,288,256]{2,1,0:T(8,128)(2,1)S(1)} %pad_maximum_fusion.1), channel_id=1, source_target_pairs={{0,8},{1,9},{2,10},{3,11},{4,12},{5,13},{6,14},{7,15},{8,0},{9,1},... | collective-permute-start | bytes 884744 | tf_op jit(solution)/shard_map/ppermute | solution.py:896
  18.8 5.7 %collective-permute-start.3 = (bf16[4,96,256]{2,1,0:T(8,128)(2,1)S(1)}, bf16[4,96,256]{2,1,0:T(8,128)(2,1)S(1)}, u32[]{:S(2)}, u32[]{:S(2)}) collective-permute-start(bf16[4,96,256]{2,1,0:T(8,128)(2,1)S(1)} %pad_maximum_fusion.2), channel_id=1, source_target_pairs={{0,4},{1,5},{2,6},{3,7},{4,0},{5,1},{6,2},{7,3},{8,12},{9,13},{10,... | collective-permute-start | bytes 589832 | tf_op jit(solution)/shard_map/ppermute | solution.py:896
  25.9 1.8 collective-permute-start.6
  26.0 21.0 %collective-permute-start.5 = (bf16[8,96,256]{2,1,0:T(8,128)(2,1)S(1)}, bf16[8,96,256]{2,1,0:T(8,128)(2,1)S(1)}, u32[]{:S(2)}, u32[]{:S(2)}) collective-permute-start(bf16[8,96,256]{2,1,0:T(8,128)(2,1)S(1)} %constant_dynamic-update-slice_fusion.near_ref), channel_id=1, source_target_pairs={{0,1},{1,0},{2,3},{3,2},{4,5},{5,4},{6,7},{7,6},{8,9},{9,8},{10,11... | collective-permute-start | bytes 1179656 | tf_op jit(solution)/shard_map/ppermute | solution.py:896
  27.7 19.3 %collective-permute-start.7 = (bf16[4,288,256]{2,1,0:T(8,128)(2,1)S(1)}, bf16[4,288,256]{2,1,0:T(8,128)(2,1)S(1)}, u32[]{:S(2)}, u32[]{:S(2)}) collective-permute-start(bf16[4,288,256]{2,1,0:T(8,128)(2,1)S(1)} %pad_maximum_fusion.refs_0_), channel_id=1, source_target_pairs={{0,4},{1,5},{2,6},{3,7},{4,0},{5,1},{6,2},{7,3},{8,12},{9,13},{10,... | collective-permute-start | bytes 1769480 | tf_op jit(solution)/shard_map/ppermute | solution.py:896
  29.2 20.9 %collective-permute-start.8 = (bf16[4,288,256]{2,1,0:T(8,128)(2,1)S(1)}, bf16[4,288,256]{2,1,0:T(8,128)(2,1)S(1)}, u32[]{:S(2)}, u32[]{:S(2)}) collective-permute-start(bf16[4,288,256]{2,1,0:T(8,128)(2,1)S(1)} %pad_maximum_fusion.refs_0_), channel_id=1, source_target_pairs={{0,1},{1,0},{2,3},{3,2},{4,5},{5,4},{6,7},{7,6},{8,9},{9,8},{10,11... | collective-permute-start | bytes 1769480 | tf_op jit(solution)/shard_map/ppermute | solution.py:896
  50.1 6.4 %collective-permute-start.10 = (bf16[8,96,256]{2,1,0:T(8,128)(2,1)S(1)}, bf16[8,96,256]{2,1,0:T(8,128)(2,1)S(1)}, u32[]{:S(2)}, u32[]{:S(2)}) collective-permute-start(bf16[8,96,256]{2,1,0:T(8,128)(2,1)S(1)} %collective-permute-done.5.near_ref), channel_id=1, source_target_pairs={{0,2},{1,3},{2,0},{3,1},{4,6},{5,7},{6,4},{7,5},{8,10},{9,11},{10,... | collective-permute-start | bytes 1179656 | tf_op jit(solution)/shard_map/ppermute | solution.py:896
  55.1 20.7 %collective-permute-start.11 = (bf16[4,288,256]{2,1,0:T(8,128)(2,1)S(1)}, bf16[4,288,256]{2,1,0:T(8,128)(2,1)S(1)}, u32[]{:S(2)}, u32[]{:S(2)}) collective-permute-start(bf16[4,288,256]{2,1,0:T(8,128)(2,1)S(1)} %pad_maximum_fusion.refs_0_), channel_id=1, source_target_pairs={{0,2},{1,3},{2,0},{3,1},{4,6},{5,7},{6,4},{7,5},{8,10},{9,11},{10,... | collective-permute-start | bytes 1769480 | tf_op jit(solution)/shard_map/ppermute | solution.py:896
  55.2 20.2 %collective-permute-start.9 = (bf16[4,288,256]{2,1,0:T(8,128)(2,1)S(1)}, bf16[4,288,256]{2,1,0:T(8,128)(2,1)S(1)}, u32[]{:S(2)}, u32[]{:S(2)}) collective-permute-start(bf16[4,288,256]{2,1,0:T(8,128)(2,1)S(1)} %collective-permute-done.7.refs_1_), channel_id=1, source_target_pairs={{0,1},{1,0},{2,3},{3,2},{4,5},{5,4},{6,7},{7,6},{8,9},{9,8},{10,11... | collective-permute-start | bytes 1769480 | tf_op jit(solution)/shard_map/ppermute | solution.py:896
  55.2 20.6 %collective-permute-start.12 = (bf16[4,288,256]{2,1,0:T(8,128)(2,1)S(1)}, bf16[4,288,256]{2,1,0:T(8,128)(2,1)S(1)}, u32[]{:S(2)}, u32[]{:S(2)}) collective-permute-start(bf16[4,288,256]{2,1,0:T(8,128)(2,1)S(1)} %collective-permute-done.7.refs_1_), channel_id=1, source_target_pairs={{0,2},{1,3},{2,0},{3,1},{4,6},{5,7},{6,4},{7,5},{8,10},{9,11},{10,... | collective-permute-start | bytes 1769480 | tf_op jit(solution)/shard_map/ppermute | solution.py:896
  55.7 20.2 %collective-permute-start.13 = (bf16[4,288,256]{2,1,0:T(8,128)(2,1)S(1)}, bf16[4,288,256]{2,1,0:T(8,128)(2,1)S(1)}, u32[]{:S(2)}, u32[]{:S(2)}) collective-permute-start(bf16[4,288,256]{2,1,0:T(8,128)(2,1)S(1)} %collective-permute-done.8.refs_2_), channel_id=1, source_target_pairs={{0,2},{1,3},{2,0},{3,1},{4,6},{5,7},{6,4},{7,5},{8,10},{9,11},{10,... | collective-permute-start | bytes 1769480 | tf_op jit(solution)/shard_map/ppermute | solution.py:896
  73.2 1.2 copy-start.1
  74.3 1.1 copy-start.3
  75.5 2.0 collective-permute-start.14
  113.4 19.8 %collective-permute-start.15 = (bf16[4640,256]{1,0:T(8,128)(2,1)}, bf16[4640,256]{1,0:T(8,128)(2,1)S(1)}, u32[]{:S(2)}, u32[]{:S(2)}) collective-permute-start(bf16[4640,256]{1,0:T(8,128)(2,1)} %get-tuple-element.172), channel_id=1, source_target_pairs={{0,2},{1,3},{2,0},{3,1},{4,6},{5,7},{6,4},{7,5},{8,10},{9,11},{10,... | collective-permute-start | bytes 7127048 | tf_op jit(solution)/shard_map/ppermute | solution.py:896
  113.8 1.4 copy-start
  115.2 1.4 copy-start.2
  116.6 1.4 copy-start.4
  118.0 15.1 %copy-start.7 = (bf16[4608,256]{1,0:T(8,128)(2,1)S(1)}, bf16[4608,256]{1,0:T(8,128)(2,1)}, u32[]{:S(2)}) copy-start(bf16[4608,256]{1,0:T(8,128)(2,1)} %get-tuple-element.170.keep_ref) | copy-start | bytes 7077892
  133.7 39.8 %collective-permute-start.16 = (bf16[1184,256]{1,0:T(8,128)(2,1)S(1)}, bf16[1184,256]{1,0:T(8,128)(2,1)S(1)}, u32[]{:S(2)}, u32[]{:S(2)}) collective-permute-start(bf16[1184,256]{1,0:T(8,128)(2,1)S(1)} %get-tuple-element.181), channel_id=1, source_target_pairs={{0,1},{1,0},{2,3},{3,2},{4,5},{5,4},{6,7},{7,6},{8,9},{9,8},{10,11... | collective-permute-start | bytes 1818632 | tf_op jit(solution)/shard_map/ppermute | solution.py:896
  143.4 30.1 %collective-permute-start.17 = (bf16[1184,256]{1,0:T(8,128)(2,1)S(1)}, bf16[1184,256]{1,0:T(8,128)(2,1)S(1)}, u32[]{:S(2)}, u32[]{:S(2)}) collective-permute-start(bf16[1184,256]{1,0:T(8,128)(2,1)S(1)} %get-tuple-element.182), channel_id=1, source_target_pairs={{0,4},{1,5},{2,6},{3,7},{4,0},{5,1},{6,2},{7,3},{8,12},{9,13},{10,... | collective-permute-start | bytes 1818632 | tf_op jit(solution)/shard_map/ppermute | solution.py:896
  144.7 28.8 %collective-permute-start.18 = (bf16[1184,256]{1,0:T(8,128)(2,1)S(1)}, bf16[1184,256]{1,0:T(8,128)(2,1)S(1)}, u32[]{:S(2)}, u32[]{:S(2)}) collective-permute-start(bf16[1184,256]{1,0:T(8,128)(2,1)S(1)} %get-tuple-element.183), channel_id=1, source_target_pairs={{0,5},{1,4},{2,7},{3,6},{4,1},{5,0},{6,3},{7,2},{8,13},{9,12},{10,... | collective-permute-start | bytes 1818632 | tf_op jit(solution)/shard_map/ppermute | solution.py:896
  173.8 28.6 %collective-permute-start.20 = (bf16[320,256]{1,0:T(8,128)(2,1)S(1)}, bf16[320,256]{1,0:T(8,128)(2,1)S(1)}, u32[]{:S(2)}, u32[]{:S(2)}) collective-permute-start(bf16[320,256]{1,0:T(8,128)(2,1)S(1)} %get-tuple-element.208), channel_id=1, source_target_pairs={{0,8},{1,9},{2,10},{3,11},{4,12},{5,13},{6,14},{7,15},{8,0},{9,1},... | collective-permute-start | bytes 491528 | tf_op jit(solution)/shard_map/ppermute | solution.py:896
  174.5 27.9 %collective-permute-start.21 = (bf16[320,256]{1,0:T(8,128)(2,1)S(1)}, bf16[320,256]{1,0:T(8,128)(2,1)S(1)}, u32[]{:S(2)}, u32[]{:S(2)}) collective-permute-start(bf16[320,256]{1,0:T(8,128)(2,1)S(1)} %get-tuple-element.209), channel_id=1, source_target_pairs={{0,16},{1,17},{2,18},{3,19},{4,20},{5,21},{6,22},{7,23},{8,24},{9,... | collective-permute-start | bytes 491528 | tf_op jit(solution)/shard_map/ppermute | solution.py:896
  184.8 17.7 %collective-permute-start.22 = (bf16[320,256]{1,0:T(8,128)(2,1)S(1)}, bf16[320,256]{1,0:T(8,128)(2,1)S(1)}, u32[]{:S(2)}, u32[]{:S(2)}) collective-permute-start(bf16[320,256]{1,0:T(8,128)(2,1)S(1)} %get-tuple-element.210), channel_id=1, source_target_pairs={{0,24},{1,25},{2,26},{3,27},{4,28},{5,29},{6,30},{7,31},{8,16},{9,... | collective-permute-start | bytes 491528 | tf_op jit(solution)/shard_map/ppermute | solution.py:896
  186.1 18.7 %collective-permute-start.19 = (bf16[3,512,256]{2,1,0:T(8,128)(2,1)S(1)}, bf16[3,512,256]{2,1,0:T(8,128)(2,1)S(1)}, u32[]{:S(2)}, u32[]{:S(2)}) collective-permute-start(bf16[3,512,256]{2,1,0:T(8,128)(2,1)S(1)} %slice_bitcast_fusion), channel_id=1, source_target_pairs={{0,1},{1,0},{2,3},{3,2},{4,5},{5,4},{6,7},{7,6},{8,9},{9,8},{10,11... | collective-permute-start | bytes 2359304 | tf_op jit(solution)/shard_map/ppermute | solution.py:896
  187.6 17.2 %copy-start.10 = (f32[16,512]{1,0:T(8,128)S(1)}, f32[16,512]{1,0:T(8,128)}, u32[]{:S(2)}) copy-start(f32[16,512]{1,0:T(8,128)} %get-tuple-element.135.table_ref) | copy-start | bytes 98308
  205.0 4.7 %collective-permute-start.23 = (bf16[784,256]{1,0:T(8,128)(2,1)S(1)}, bf16[784,256]{1,0:T(8,128)(2,1)S(1)}, u32[]{:S(2)}, u32[]{:S(2)}) collective-permute-start(bf16[784,256]{1,0:T(8,128)(2,1)S(1)} %get-tuple-element.215), channel_id=1, source_target_pairs={{0,2},{1,3},{2,0},{3,1},{4,6},{5,7},{6,4},{7,5},{8,10},{9,11},{10,... | collective-permute-start | bytes 1204232 | tf_op jit(solution)/shard_map/ppermute | solution.py:896
  205.1 3.7 %collective-permute-start.24 = (bf16[16,256]{1,0:T(8,128)(2,1)S(1)}, bf16[16,256]{1,0:T(8,128)(2,1)S(1)}, u32[]{:S(2)}, u32[]{:S(2)}) collective-permute-start(bf16[16,256]{1,0:T(8,128)(2,1)S(1)} %get-tuple-element.216), channel_id=1, source_target_pairs={{0,1},{1,0},{2,3},{3,2},{4,5},{5,4},{6,7},{7,6},{8,9},{9,8},{10,11... | collective-permute-start | bytes 24584 | tf_op jit(solution)/shard_map/ppermute | solution.py:896
  206.6 3.1 %collective-permute-start.25 = (bf16[16,256]{1,0:T(8,128)(2,1)S(1)}, bf16[16,256]{1,0:T(8,128)(2,1)S(1)}, u32[]{:S(2)}, u32[]{:S(2)}) collective-permute-start(bf16[16,256]{1,0:T(8,128)(2,1)S(1)} %get-tuple-element.216), channel_id=1, source_target_pairs={{0,3},{1,2},{2,1},{3,0},{4,7},{5,6},{6,5},{7,4},{8,11},{9,10},{10,... | collective-permute-start | bytes 24584 | tf_op jit(solution)/shard_map/ppermute | solution.py:896
  209.7 1.9 copy-start.6
  209.7 2.4 %copy-start.8 = (f32[1536,512]{1,0:T(8,128)S(1)}, f32[1536,512]{1,0:T(8,128)}, u32[]{:S(2)}) copy-start(f32[1536,512]{1,0:T(8,128)} %get-tuple-element.218.gh_ref) | copy-start | bytes 9437188
  209.8 7.2 %collective-permute-start.26 = (bf16[400,256]{1,0:T(8,128)(2,1)S(1)}, bf16[400,256]{1,0:T(8,128)(2,1)S(1)}, u32[]{:S(2)}, u32[]{:S(2)}) collective-permute-start(bf16[400,256]{1,0:T(8,128)(2,1)S(1)} %get-tuple-element.217), channel_id=1, source_target_pairs={{0,4},{1,5},{2,6},{3,7},{4,0},{5,1},{6,2},{7,3},{8,12},{9,13},{10,... | collective-permute-start | bytes 614408 | tf_op jit(solution)/shard_map/ppermute | solution.py:896
  217.1 4.9 %collective-permute-start.27 = (bf16[112,256]{1,0:T(8,128)(2,1)S(1)}, bf16[112,256]{1,0:T(8,128)(2,1)S(1)}, u32[]{:S(2)}, u32[]{:S(2)}) collective-permute-start(bf16[112,256]{1,0:T(8,128)(2,1)S(1)} %get-tuple-element.233), channel_id=1, source_target_pairs={{0,8},{1,9},{2,10},{3,11},{4,12},{5,13},{6,14},{7,15},{8,0},{9,1},... | collective-permute-start | bytes 172040 | tf_op jit(solution)/shard_map/ppermute | solution.py:896
  217.7 7.1 %collective-permute-start.28 = (bf16[112,256]{1,0:T(8,128)(2,1)S(1)}, bf16[112,256]{1,0:T(8,128)(2,1)S(1)}, u32[]{:S(2)}, u32[]{:S(2)}) collective-permute-start(bf16[112,256]{1,0:T(8,128)(2,1)S(1)} %get-tuple-element.234), channel_id=1, source_target_pairs={{0,16},{1,17},{2,18},{3,19},{4,20},{5,21},{6,22},{7,23},{8,24},{9,... | collective-permute-start | bytes 172040 | tf_op jit(solution)/shard_map/ppermute | solution.py:896
  220.2 6.0 %collective-permute-start.29 = (bf16[112,256]{1,0:T(8,128)(2,1)S(1)}, bf16[112,256]{1,0:T(8,128)(2,1)S(1)}, u32[]{:S(2)}, u32[]{:S(2)}) collective-permute-start(bf16[112,256]{1,0:T(8,128)(2,1)S(1)} %get-tuple-element.235), channel_id=1, source_target_pairs={{0,24},{1,25},{2,26},{3,27},{4,28},{5,29},{6,30},{7,31},{8,16},{9,... | collective-permute-start | bytes 172040 | tf_op jit(solution)/shard_map/ppermute | solution.py:896
where the time goes:
time: 224 us; the launch traced here: 227 us
  Pallas kernels  137 us (61%)
  starting transfers between devices  54.5 us (24%)
  waiting for transfers between devices  26.1 us (12%)
  local copies, waits for them, and re-layouts  7.82 us (3%)
    pallas_call x3, Pallas kernels, attend_backward_fast(): pl.pallas_call(functools.partial(backward_kernel, first), grid=(pairs, ro...  58.4 us
    ppermute x30, starting transfers between devices, swap(): lax.ppermute(values, ('dp', 'head'), [(i, i ^ mask) for i in range(device...  54.5 us
    pallas_call x1, Pallas kernels, middle(): pl.pallas_call(functools.partial(middle_kernel, masks), grid=(rows // til...  35.9 us
    pallas_call x2, Pallas kernels, attend_forward_fast(): pl.pallas_call(functools.partial(forward_kernel, side_at), grid=(pairs, r...  32.9 us
    ppermute x30, waiting for transfers between devices, swap(): lax.ppermute(values, ('dp', 'head'), [(i, i ^ mask) for i in range(device...  26.1 us
    unnamed x29, local copies, waits for them, and re-layouts  7.76 us
    pallas_call x1, Pallas kernels, input_grads(): pl.pallas_call(input_grad_kernel, grid=(rows // tile,), in_specs=[wide, w...  4.66 us
  transfers between devices with their start and end apart: 30, of which 16 were waited for; matrix products, arithmetic and copies ran while one was open for 0% of the time, Pallas kernels for 43%

commit v1 on v0

--- a/solution.py
+++ b/solution.py
@@ -400,9 +400,9 @@
     )(live, language, task, *rest)
 
 
-def real_rows(x_ref):
-    row = pl.program_id(0) * x_ref.shape[0] + lax.broadcasted_iota(jnp.int32, x_ref.shape, 0)
-    return row < FRAMES
+def real_rows(x_ref, first=0):
+    tile = pl.program_id(0) + first
+    return tile * x_ref.shape[0] + lax.broadcasted_iota(jnp.int32, x_ref.shape, 0) < FRAMES
 
 
 def unit_rows(values):
@@ -426,7 +426,7 @@
 
 def first_norm(frames, table):
     width = frames.shape[1]
-    tile = 512
+    tile = 256
     return pl.pallas_call(
         norm_kernel,
         grid=(PADDED // tile,),
@@ -453,8 +453,9 @@
 
 def forward_kernel(side_at, n_ref, near_ref, far_ref, table_ref, *refs):
     (
-        q_ref, k_ref, v_ref, p_ref, c_ref, inv_ref, row_ref, w_ref, keys_ref, vt_ref, small_ref
-    ) = refs[-11:]
+        q_ref, k_ref, v_ref, p_ref, c_ref, rest_ref, inv_ref, w_ref,
+        keys_ref, vt_ref, both_ref, small_ref,
+    ) = refs[-12:]
     pair, step = pl.program_id(0), pl.program_id(1)
     count, rows3, half = near_ref.shape
     rows = rows3 // 3
@@ -480,62 +481,67 @@
         queries = q_ref[...].astype(F32)
         high = keys.astype(BF16).astype(F32)
         flipped = v_ref[...].astype(F32).T
+        spare = vt_ref.shape[1] - HEAD_DIM
         shape = (vt_ref.shape[1], flipped.shape[1])
         real = lax.broadcasted_iota(jnp.int32, shape, 1) < FRAMES
         first = lax.broadcasted_iota(jnp.int32, shape, 0) == HEAD_DIM
-        small = None
+        shape = (LANES, LANES)
+        one, two = (lax.broadcasted_iota(jnp.int32, shape, j) < HEAD_DIM for j in (0, 1))
+        same = jnp.where(one == two, 1.0, 0.0).astype(BF16)
+        norms = [
+            jnp.max(dot_on((m * m).astype(BF16), same, 1, 0), axis=0, keepdims=True)
+            for m in (queries, keys)
+        ]
+        bound = jnp.max(norms[0] * norms[1])
+        small_ref[0] = (bound < 90.0 * 90.0).astype(jnp.int32)
         for h in (0, 1):
             keys_ref[h, :, 0:LANES] = masked(high, h).astype(BF16)
             keys_ref[h, :, LANES:] = masked(keys - high, h).astype(BF16)
             mine = flipped[HEAD_DIM * h : HEAD_DIM * (h + 1), :]
-            mine = jnp.concatenate([mine, mine[0 : shape[0] - HEAD_DIM]], axis=0)
+            mine = jnp.concatenate([mine, mine[0:spare]], axis=0)
             vt_ref[h] = jnp.where(real, jnp.where(first, 1.0, mine), 0.0).astype(BF16)
-            norms = [
-                jnp.max(jnp.sum(masked(m * m, h), axis=1, keepdims=True)) for m in (queries, keys)
-            ]
-            fits = (norms[0] < 1e18) & (norms[1] < 1e18) & (norms[0] * norms[1] < 50.0 * 50.0)
-            small = fits if small is None else small & fits
-        small_ref[0] = small.astype(jnp.int32)
 
     tile = c_ref.shape[0]
     tail = FRAMES // 16 * 16
 
-    def attend(start, size, at, shift):
+    def attend(h, start, size, at, shift):
         queries = q_ref[pl.ds(start, size), :]
-        queries = jnp.concatenate([queries, queries], axis=1)
-        contexts, inverses = [], []
-        for h in (0, 1):
-            scores = dot_on(keys_ref[h], queries, 1, 1)
-            if shift:
-                real = lax.broadcasted_iota(jnp.int32, scores.shape, 0) < FRAMES
-                scores = jnp.where(real, scores, -1e30)
-                scores = scores - jnp.max(scores, axis=0, keepdims=True)
-            probs = jnp.exp2(scores)
-            low = probs.astype(BF16)
-            p_ref[h, 0:tail, at] = low[0:tail]
-            last = probs[tail:]
-            real = lax.broadcasted_iota(jnp.int32, last.shape, 0) < FRAMES - tail
-            p_ref[h, tail:, at] = jnp.where(real, last, 0.0).astype(BF16)
-            summed = dot_on(vt_ref[h], low, 1, 0)
-            inverse = 1.0 / summed[HEAD_DIM : HEAD_DIM + 1, :]
-            row_ref[h : h + 1, at] = inverse
-            contexts.append(summed[0:HEAD_DIM, :] * inverse)
-            inverses.append(jnp.broadcast_to(inverse, (HEAD_DIM, inverse.shape[1])))
-        return jnp.concatenate(contexts, axis=0).T.astype(BF16), jnp.concatenate(inverses, axis=0).T
+        scores = dot_on(keys_ref[h], jnp.concatenate([queries, queries], axis=1), 1, 1)
+        if shift:
+            real = lax.broadcasted_iota(jnp.int32, scores.shape, 0) < FRAMES
+            scores = jnp.where(real, scores, -1e30)
+            scores = scores - jnp.max(scores, axis=0, keepdims=True)
+        probs = jnp.exp2(scores)
+        low = probs.astype(BF16)
+        p_ref[h, 0:tail, at] = low[0:tail]
+        last = probs[tail:]
+        real = lax.broadcasted_iota(jnp.int32, last.shape, 0) < FRAMES - tail
+        p_ref[h, tail:, at] = jnp.where(real, last, 0.0).astype(BF16)
+        summed = dot_on(vt_ref[h], low, 1, 0)
+        inverse = 1.0 / summed[HEAD_DIM : HEAD_DIM + 1, :]
+        both_ref[0, h, :, at] = summed[0:HEAD_DIM, :] * inverse
+        both_ref[1, h, :, at] = jnp.broadcast_to(inverse, (HEAD_DIM, inverse.shape[1]))
 
     @pl.when(small_ref[0] == 1)
     def _():
-        c_ref[...], inv_ref[...] = attend(step * tile, tile, slice(0, tile), False)
+        for h in (0, 1):
+            attend(h, step * tile, tile, slice(0, tile), False)
 
     @pl.when(small_ref[0] == 0)
     def _():
-        size = 2 * LANES
-
-        @pl.loop(0, tile // size)
+        size = LANES
+
+        @pl.loop(0, 2 * tile // size)
         def _(t):
+            h, t = t & 1, t >> 1
             at = pl.ds(pl.multiple_of(t * size, size), size)
-            start = pl.multiple_of(step * tile + t * size, size)
-            c_ref[at, :], inv_ref[at, :] = attend(start, size, at, True)
+            attend(h, pl.multiple_of(step * tile + t * size, size), size, at, True)
+
+    context = both_ref[0].reshape(LANES, tile).T
+    low = context.astype(BF16)
+    c_ref[...] = low
+    rest_ref[...] = (context - low.astype(F32)).astype(BF16)
+    inv_ref[...] = both_ref[1].reshape(LANES, tile).T
 
 
 def attend_forward_fast(side_at, normed, near, far, table, before=()):
@@ -555,21 +561,20 @@
         out_specs=[
             full, full, full,
             pl.BlockSpec((2, rows, tile), lambda p, i: (p + at, 0, i)),
-            block, block,
-            pl.BlockSpec((None, 8, tile), lambda p, i: (p + at, 0, i)),
-            weights,
+            block, block, block, weights,
         ],
         out_shape=[struct((rows, width), BF16)] * 3
         + [
             struct((width // HEAD_DIM, rows, rows), BF16),
-            struct((rows, width), BF16),
+            pltpu.HBM((rows, width), BF16),
+            pltpu.HBM((rows, width), BF16),
             struct((rows, width), F32),
-            struct((width // LANES, 8, rows), F32),
-            struct((3, width, width), BF16),
+            pltpu.HBM((3, width, width), BF16),
         ],
         scratch_shapes=[
             pltpu.VMEM((2, rows, 2 * LANES), BF16),
             pltpu.VMEM((2, HEAD_DIM + 16, rows), BF16),
+            pltpu.VMEM((2, 2, HEAD_DIM, tile), F32),
             pltpu.SMEM((1,), jnp.int32),
         ],
         input_output_aliases={4 + j: j for j in range(len(before))},
@@ -579,7 +584,8 @@
 
 
 def backward_kernel(
-    first, q_ref, k_ref, v_ref, p_ref, inv_ref, row_ref, c_ref, g_ref, nt_ref, w_ref, vec_in_ref, *refs
+    first, q_ref, k_ref, v_ref, p_ref, inv_ref, c_ref, rest_ref, g_ref, nt_ref, w_ref,
+    vec_in_ref, *refs
 ):
     dq_ref, dk_ref, dv_ref, dw_ref, vec_ref, vals_ref, kt_ref, acck, accv, acc_one, acc_two = refs[-11:]
     pair, step = pl.program_id(0), pl.program_id(1)
@@ -596,21 +602,20 @@
 
     tile = q_ref.shape[0]
     plain = q_ref[...].astype(F32)
-    grads = g_ref[...].astype(F32)
-    products = (grads * c_ref[...].astype(F32)).T
-    divided = grads * inv_ref[...]
-    diffs, queries, outers, flipped = [], [], [], []
+    divided = g_ref[...].astype(F32) * inv_ref[...]
+    low = divided.astype(BF16)
+    divided = low.astype(F32)
+    products = (divided * (c_ref[...].astype(F32) + rest_ref[...].astype(F32))).T
+    diffs, queries, flipped = [], [], []
     for h in (0, 1):
         rows = slice(HEAD_DIM * h, HEAD_DIM * (h + 1))
         row_delta = jnp.sum(products[rows], axis=0, keepdims=True)
-        grad_probs = dot_on(vals_ref[h], g_ref[...], 1, 1)
-        scaled = (grad_probs - row_delta) * row_ref[h : h + 1, :]
-        diff = (p_ref[h].astype(F32) * scaled).astype(BF16)
+        accv[...] += dot_on(p_ref[h], masked(divided, h).astype(BF16), 1, 0)
+        grad_probs = dot_on(vals_ref[h], low, 1, 1)
+        diff = p_ref[h] * (grad_probs - row_delta).astype(BF16)
         diffs.append(diff)
-        outers.append(masked(divided, h).astype(BF16))
         queries.append(masked(plain, h).astype(BF16))
         flipped.append(dot_on(kt_ref[rows, :], diff, 1, 0))
-    accv[...] += dot_on(p_ref[0], outers[0], 1, 0) + dot_on(p_ref[1], outers[1], 1, 0)
     acck[...] += dot_on(diffs[0], queries[0], 1, 0) + dot_on(diffs[1], queries[1], 1, 0)
     at = pl.ds(pl.multiple_of(step * tile, tile), tile)
     dq_ref[at, :] = (jnp.concatenate(flipped, axis=0) * 0.125).T.astype(BF16)
@@ -626,8 +631,11 @@
         dk_ref[...] = (acck[...] * 0.125).astype(BF16)
         dv_ref[...] = accv[...].astype(BF16)
         columns = pl.ds(pl.multiple_of((pair + first) * LANES, LANES), LANES)
+        both = jnp.concatenate([dq_ref[...], dk_ref[...]], axis=1)
+        both = dot_on(nt_ref[...], both, 1, 0)
+        products = [both[:, 0:LANES], both[:, LANES:], dot_on(nt_ref[...], dv_ref[...], 1, 0)]
         for j, ref in enumerate((dq_ref, dk_ref, dv_ref)):
-            dw = dot_on(nt_ref[...], ref[...], 1, 0)
+            dw = products[j]
             dw_ref[j] = dw.astype(dw_ref.dtype)
             column_sums = jnp.sum(ref[...].astype(F32), axis=0, keepdims=True)
             weights = w_ref[j].astype(F32)
@@ -643,12 +651,14 @@
 
 
 def attend_backward_fast(
-    first, pairs, q, k, v, probs, inverse, rows_inverse, context, grads, normed_t, weights, vec,
-    before=(),
+    first, pairs, q, k, v, probs, inverse, context, rest, grads, normed_t, weights, vec, before=()
 ):
     rows, width = q.shape
     half = width // 2
-    tile = 512
+    context, rest, grads, weights = (
+        pltpu.with_memory_space_constraint(x, pltpu.HBM) for x in (context, rest, grads, weights)
+    )
+    tile = 384 if pairs > 1 else 256
     block = pl.BlockSpec((tile, LANES), lambda p, i: (i, p + first))
     full = pl.BlockSpec((rows, LANES), lambda p, i: (0, p + first))
     gradient = pl.BlockSpec(
@@ -657,9 +667,7 @@
     in_specs = [
         block, full, full,
         pl.BlockSpec((2, rows, tile), lambda p, i: (p + first, 0, i)),
-        block,
-        pl.BlockSpec((None, 8, tile), lambda p, i: (p + first, 0, i)),
-        block, block, whole(normed_t.shape),
+        block, block, block, block, whole(normed_t.shape),
         pl.BlockSpec((3, width, LANES), lambda p, i: (0, 0, p + first)),
         whole(vec.shape),
     ]
@@ -682,7 +690,7 @@
         input_output_aliases={count + j: j for j in range(len(before))},
         name="attend_backward",
         **params(14 * pairs, 34),
-    )(q, k, v, probs, inverse, rows_inverse, context, grads, normed_t, weights, vec, *before)
+    )(q, k, v, probs, inverse, context, rest, grads, normed_t, weights, vec, *before)
 
 
 def middle_kernel(masks, c_ref, x_ref, cot_ref, table_ref, *refs):
@@ -698,14 +706,16 @@
     ow = width // (devices // 2)
     ff = (piece_rows - ow) // 4
     hidden_all = devices * ff
-    chunk = 512
+    chunk = 1024
     chunks = hidden_all // chunk
 
     @pl.when(step == 0)
     def _():
         for mask, ref in zip(masks, pieces):
-            for t in range(layers):
-                owner = (dp * 2 + side) ^ (mask + (t & 1) * 2 * BIT_Z + (t & 2) // 2 * BIT_Z)
+
+            @pl.loop(0, layers)
+            def _(t, mask=mask, ref=ref):
+                owner = (dp * 2 + side) ^ (mask + (t & 1) * 2 * BIT_Z + (t >> 1) * BIT_Z)
                 rows = pl.ds(pl.multiple_of(owner * ff, ff), ff)
                 down_n[rows, 0:half] = ref[t, 0:ff, :]
                 down_n[rows, half:] = ref[t, ff : 2 * ff, :]
@@ -714,17 +724,24 @@
                 rows = pl.ds(pl.multiple_of((owner >> 1) * ow, ow), ow)
                 at = slice(0, half) if mask & BIT_X else slice(half, width)
                 out_t[rows, at] = ref[t, 4 * ff :, :]
-        for j in range(chunks):
-            rows = slice(j * chunk, (j + 1) * chunk)
+
+        @pl.loop(0, hidden_all // width)
+        def _(j):
+            rows = pl.ds(pl.multiple_of(j * width, width), width)
             up_n[:, rows] = up_t[rows, :].T
             down_t[:, rows] = down_n[rows, :].T
-            bias = table_ref[UP_BIAS + j : UP_BIAS + j + 1, :]
-            upb_t[rows, :] = jnp.broadcast_to(bias, (LANES, chunk)).T
-        acc_up[...] = jnp.zeros_like(acc_up)
-        acc_down[...] = jnp.zeros_like(acc_down)
-        acc_out[...] = jnp.zeros_like(acc_out)
-        acc_upb[...] = jnp.zeros_like(acc_upb)
+            bias = table_ref[pl.ds(UP_BIAS + j, 1), :]
+            upb_t[rows, :] = jnp.broadcast_to(bias, (LANES, width)).T
+            acc_upb[rows, :] = jnp.zeros((width, LANES), F32)
+
+        @pl.loop(0, acc_out.shape[0])
+        def _(j):
+            acc_out[j] = jnp.zeros(acc_out.shape[1:], F32)
+
         acc_vec[...] = jnp.zeros_like(acc_vec)
+
+    def add_to(ref, at, values):
+        ref[at] = jnp.where(step == 0, 0.0, ref[at]) + values
 
     def row_of(j):
         return table_ref[j : j + 1, :]
@@ -747,14 +764,14 @@
         slope = bell + pre * (jnp.exp2(pre * pre * (-0.5 * LOG2E)) * 0.3989422804014327)
         activated = (pre * bell).astype(BF16)
         result_t += dot_on(down_t[:, rows], activated, 1, 0)
-        acc_down[slots] += dot_on(activated, grad_two, 1, 0).reshape(-1, ff, width)
+        add_to(acc_down, slots, dot_on(activated, grad_two, 1, 0).reshape(-1, ff, width))
         grad_pre = (dot_on(down_n[rows, :], grad_two, 1, 1) * slope).astype(BF16)
         rounded = grad_pre.astype(F32)
         partial = rounded[:, 0:LANES]
         for lanes in range(LANES, tile, LANES):
             partial += rounded[:, lanes : lanes + LANES]
         acc_upb[rows, :] += partial
-        acc_up[slots] += dot_on(grad_pre, normed, 1, 0).reshape(-1, ff, width)
+        add_to(acc_up, slots, dot_on(grad_pre, normed, 1, 0).reshape(-1, ff, width))
         grad_normed_t += dot_on(up_n[:, rows], grad_pre, 1, 0)
     result = hidden + result_t.T + row_of(DOWN_BIAS)
     out_ref[...] = (result * row_of(LIVE)).astype(BF16)
@@ -773,17 +790,23 @@
     def _():
         targets = devices // 2
         for ref, bit in ((keep_ref, core), (send_ref, 1 - core)):
-            for t in range(targets):
-                y, x, z = t // (2 * LAYERS), t // LAYERS % 2, t % LAYERS
-                at = t * piece_rows
+
+            @pl.loop(0, targets)
+            def _(t, ref=ref, bit=bit):
+                y, x, z = t >> 3, (t >> 2) & 1, t & 3
                 chip = z * 2 + y
                 slot = chip * 4 + bit * 2 + x
                 near = pl.ds(pl.multiple_of((1 - (side ^ x)) * half, half), half)
-                ref[at : at + ff, :] = acc_down[slot, :, 0:half].astype(BF16)
-                ref[at + ff : at + 2 * ff, :] = acc_down[slot, :, half:].astype(BF16)
-                ref[at + 2 * ff : at + 3 * ff, :] = acc_up[slot, :, 0:half].astype(BF16)
-                ref[at + 3 * ff : at + 4 * ff, :] = acc_up[slot, :, half:].astype(BF16)
-                ref[at + 4 * ff : at + piece_rows, :] = acc_out[chip * 2 + bit, :, near].astype(BF16)
+
+                def rows(j, count=ff):
+                    return pl.ds(pl.multiple_of(t * piece_rows + j * ff, 32), count)
+
+                ref[rows(0), :] = acc_down[slot, :, 0:half].astype(BF16)
+                ref[rows(1), :] = acc_down[slot, :, half:].astype(BF16)
+                ref[rows(2), :] = acc_up[slot, :, 0:half].astype(BF16)
+                ref[rows(3), :] = acc_up[slot, :, half:].astype(BF16)
+                ref[rows(4, ow), :] = acc_out[chip * 2 + bit, :, near].astype(BF16)
+
         for j in range(4):
             total = jnp.sum(acc_vec[8 * j : 8 * j + 8, :], axis=0, keepdims=True)
             vec_ref[2 * j : 2 * j + 1, :] = total[:, 0:half]
@@ -797,6 +820,9 @@
 
 
 def middle(context, frames, cotangent, table, masks, pieces):
+    context, frames, cotangent = (
+        pltpu.with_memory_space_constraint(x, pltpu.HBM) for x in (context, frames, cotangent)
+    )
     rows, width = context.shape
     layers, piece_rows, half = pieces[0].shape
     devices = layers * len(masks)
@@ -813,8 +839,8 @@
         out_specs=[wide, wide, wide, whole((body + 32, half)), whole((body, half)), whole((16, half))],
         out_shape=[
             struct(frames.shape, BF16),
-            struct((rows, width), BF16),
-            struct((rows, width), F32),
+            pltpu.HBM((rows, width), BF16),
+            pltpu.HBM((rows, width), F32),
             struct((body + 32, half), BF16),
             struct((body, half), BF16),
             struct((16, half), F32),
@@ -833,7 +859,7 @@
             pltpu.VMEM((32, width), F32),
         ],
         name="middle",
-        **params(38, 48),
+        **params(38, 40),
     )(context, frames, cotangent, table, *pieces)
 
 
@@ -859,19 +885,26 @@
         vec += load_two(ref, ref.shape[0] - 2 * vec_rows, vec_rows)
     sum_ref[...] = vec
 
-    def total(part):
-        rows = pl.ds(pl.multiple_of(part * size, 32), size)
+    own = masks[0](dp, side)
+    block = 96
+
+    def total(part, at):
+        rows = pl.ds(pl.multiple_of(part * size + at, 32), block)
         values = keep_ref[rows, :].astype(F32)
         for ref in came:
             if ref.shape[0] > 2 * vec_rows:
                 values += ref[rows, :].astype(F32)
         return values
 
-    own = masks[0](dp, side)
-    mine_ref[...] = total(own)
-    for mask, ref in zip(masks[1:], sends):
-        if mask is not None:
-            ref[0:size, :] = total(own ^ mask).astype(BF16)
+    @pl.loop(0, size // block)
+    def _(t):
+        at = pl.multiple_of(t * block, 32)
+        mine_ref[pl.ds(at, block), :] = total(own, at)
+        for mask, ref in zip(masks[1:], sends):
+            if mask is not None:
+                ref[pl.ds(at, block), :] = total(own ^ mask, at).astype(BF16)
+
+    for ref in sends:
         store_two(ref, ref.shape[0] - 2 * vec_rows, vec)
 
 
@@ -900,28 +933,36 @@
     return ((dp >> 1) & 1) * 2 + side
 
 
-def part_y(dp, side):
-    return (dp >> 1) & 1
+def part_yz(dp, side):
+    return ((dp >> 1) & 1) * 2 + ((dp >> 2) & 1)
 
 
 def part_z(dp, side):
     return dp >> 2
 
 
-def gather_kernel(table_ref, dw_ref, got_ref, vec_in_ref, send_ref, keep_ref, vec_ref, vsend_ref):
+def part_high(dp, side):
+    return dp >> 3
+
+
+def gather_kernel(table_ref, dw_ref, got_ref, vec_in_ref, send_ref, keep_ref, vec_ref):
     dp, side = place()
     core = lax.rem(dp, 2)
     width = table_ref.shape[1]
     half = width // 2
     ow = width // 16
     for ref, bit in ((keep_ref, core), (send_ref, 1 - core)):
-        for t in range(2 * LAYERS):
-            chip = t % LAYERS * 2 + t // LAYERS
+
+        @pl.loop(0, 2 * LAYERS)
+        def _(t, ref=ref, bit=bit):
+            z = (t & 1) * 2 + ((t >> 1) & 1)
+            chip = z * 2 + (t >> 2)
             rows = pl.ds(pl.multiple_of((chip * 2 + bit) * ow, ow), ow)
             for j in range(3):
-                at = t * 3 * ow + j * ow
+                at = pl.ds(pl.multiple_of(t * 3 * ow + j * ow, ow), ow)
                 both = dw_ref[j, rows, :].astype(F32) + got_ref[j, rows, :].astype(F32)
-                ref[at : at + ow, :] = both.astype(ref.dtype)
+                ref[at, :] = both.astype(ref.dtype)
+
     one, two = vec_in_ref[0:1, :], vec_in_ref[1:2, :]
     gain = table_ref[LN1_GAIN : LN1_GAIN + 1, :]
     offset = table_ref[LN1_OFFSET : LN1_OFFSET + 1, :]
@@ -934,14 +975,13 @@
         vec_ref[4 + 2 * j : 5 + 2 * j, :] = jnp.where(side == 0, own, other)
         vec_ref[5 + 2 * j : 6 + 2 * j, :] = jnp.where(side == 0, other, own)
     store_two(send_ref, 24 * ow, vec_ref[...])
-    store_two(vsend_ref, 0, vec_ref[...])
 
 
 def gather_grads(table, dw, got, vec):
     width = table.shape[1]
     half = width // 2
     rows = 24 * (width // 16)
-    shapes = [((rows + 16, half), BF16), ((rows, half), F32), ((8, half), F32), ((16, half), BF16)]
+    shapes = [((rows + 16, half), BF16), ((rows, half), F32), ((8, half), F32)]
     return pl.pallas_call(
         gather_kernel,
         grid=(1,),
@@ -959,15 +999,16 @@
 
 
 def finish_kernel(ff, ow, mine_ref, vec_ref, mine_w_ref, vec_w_ref, *refs):
-    came, came_w, outs = refs[: LAYERS - 1], refs[LAYERS - 1 : 2 * LAYERS - 2], refs[2 * LAYERS - 2 :]
+    came, came_w, outs = refs[: LAYERS - 1], refs[LAYERS - 1 : LAYERS + 2], refs[LAYERS + 2 :]
     down_ref, up_ref, out_ref, *outs = outs
 
     def total(mine, vec, parts):
         size = mine.shape[0]
         values, sums = mine[...], vec[...]
         for ref in parts:
-            values += ref[0:size, :].astype(F32)
-            sums += load_two(ref, size, vec.shape[0])
+            if ref.shape[0] > size:
+                values += ref[0:size, :].astype(F32)
+            sums += load_two(ref, ref.shape[0] - 2 * vec.shape[0], vec.shape[0])
         return values, sums
 
     half = mine_ref.shape[1]
@@ -1005,28 +1046,31 @@
     )(mine, vec, mine_w, vec_w, *came, *came_w)
 
 
-def input_grad_kernel(x_ref, gh_ref, table_ref, w_ref, dq_ref, dk_ref, dv_ref, gf_ref):
+def input_grad_kernel(first, x_ref, gh_ref, table_ref, w_ref, dq_ref, dk_ref, dv_ref, *refs):
+    gf_ref = refs[-1]
     total = dot_on(dq_ref[...], w_ref[0], 1, 1)
     total += dot_on(dk_ref[...], w_ref[1], 1, 1)
     total += dot_on(dv_ref[...], w_ref[2], 1, 1)
-    unit, scale = unit_rows(jnp.where(real_rows(x_ref), x_ref[...].astype(F32), 0.0))
+    unit, scale = unit_rows(jnp.where(real_rows(x_ref, first), x_ref[...].astype(F32), 0.0))
     lifted = total * table_ref[LN1_GAIN : LN1_GAIN + 1, :]
     gf_ref[...] = (gh_ref[...] + unit_back(lifted, unit, scale)).astype(BF16)
 
 
-def input_grads(frames, grad_hidden, table, weights, grads):
+def input_grads(first, tiles, frames, grad_hidden, table, weights, grads, before=()):
     rows, width = grad_hidden.shape
-    tile = 512
-    wide = pl.BlockSpec((tile, width), lambda i: (i, 0))
+    tile = 256
+    wide = pl.BlockSpec((tile, width), lambda i: (i + first, 0))
     return pl.pallas_call(
-        input_grad_kernel,
-        grid=(rows // tile,),
-        in_specs=[wide, wide, whole(table.shape), whole(weights.shape), wide, wide, wide],
+        functools.partial(input_grad_kernel, first),
+        grid=(tiles,),
+        in_specs=[wide, wide, whole(table.shape), whole(weights.shape), wide, wide, wide]
+        + [pl.BlockSpec(memory_space=pl.ANY)] * len(before),
         out_specs=wide,
         out_shape=struct(frames.shape, BF16),
+        input_output_aliases={7 + j: j for j in range(len(before))},
         name="input_grads",
-        **params(9, 20),
-    )(frames, grad_hidden, table, weights, *grads)
+        **params(tiles, 20),
+    )(frames, grad_hidden, table, weights, *grads, *before)
 
 
 def on_whole_windows(
@@ -1069,17 +1113,23 @@
     )
     together = lax.optimization_barrier
 
+    def after(values, first):
+        return together((values, first))[0]
+
     def doubled(values, came):
         return jnp.concatenate([values, came], axis=0)
 
     came = swap(pieces, 2 * BIT_Z)
     normed, normed_t = first_norm(frames, table)
-    came, normed, big = together((came, normed, big[None]))
+    came, normed = together((came, normed))
+    big = after(big[None], came)
     pieces = doubled(pieces, came)
-    came, came_big = together((swap(pieces, BIT_Z), swap(big, 2 * BIT_Z)))
-    pieces, big = doubled(pieces, came), doubled(big, came_big)
-    came, came_big = together((swap(pieces, BIT_Y), swap(big, BIT_Z)))
-    near, big = doubled(pieces, came), doubled(big, came_big)
+    big = doubled(big, swap(big, 2 * BIT_Z))
+    came = swap(pieces, BIT_Z)
+    big = after(big, came)
+    pieces = doubled(pieces, came)
+    near = doubled(pieces, swap(pieces, BIT_Y))
+    big = doubled(big, swap(big, BIT_Z))
     far = swap(near, BIT_CORE)
     near_other = swap(near, BIT_X)
 
@@ -1091,7 +1141,7 @@
     far_other = swap(near_other, BIT_CORE)
     big_xy = swap(big_y, BIT_X)
     across = [swap(p, BIT_CORE) for p in (big, big_y, big_x)]
-    q, k, v, probs, context, inverse, rows_inverse, weights = attend_forward_fast(
+    q, k, v, probs, context, rest, inverse, weights = attend_forward_fast(
         0, normed, near_other, far_other, table, half_done
     )
     big_xy, context = together((big_xy, context))
@@ -1104,8 +1154,7 @@
 
     def backward(first, pairs, grads, vec, before=()):
         return attend_backward_fast(
-            first, pairs, q, k, v, probs, inverse, rows_inverse, context, grads, normed_t, weights,
-            vec, before,
+            first, pairs, q, k, v, probs, inverse, context, rest, grads, normed_t, weights, vec, before
         )
 
     came = swap(send, BIT_CORE)
@@ -1123,15 +1172,19 @@
     came_z = [swap(s, m * BIT_Z) for s, m in zip(sends, (1, 2, 3))]
     *done, dw, vec_w = backward(3, 1, grads, vec_w, done)
 
-    came_z, vec_w = lax.optimization_barrier((came_z, vec_w))
-    send, keep_w, vec_w, vec_send = gather_grads(table, dw, got, vec_w)
-    came = [swap(send, BIT_CORE), swap(vec_send, BIT_X), swap(vec_send, BIT_X | BIT_CORE)]
-    mine_w, vec_w, send = spread(keep_w, vec_w, came, part_y, (1,), 2)
-    came = [swap(send, BIT_Y)]
-    grad_frames = input_grads(frames, grad_hidden, table, weights, done)
-    came, grad_frames = lax.optimization_barrier((came, grad_frames))
-    mine_w, vec_w, *sends = spread(mine_w, vec_w, came, part_z, (1, 2, 3), LAYERS)
-    came_w = [swap(s, m * BIT_Z) for s, m in zip(sends, (1, 2, 3))]
+    came_z, got, vec_w = together((came_z, got, vec_w))
+    send, keep_w, vec_w = gather_grads(table, dw, got, vec_w)
+    came = [swap(send, BIT_CORE)]
+    mine_w, vec_w, *sends = spread(keep_w, vec_w, came, part_yz, (1, 2, 3), 4)
+    came = [swap(s, m) for s, m in zip(sends, (BIT_Z, BIT_Y, BIT_Z | BIT_Y))]
+    grad_frames = input_grads(0, 4, frames, grad_hidden, table, weights, done)
+    came, grad_frames = together((came, grad_frames))
+    mine_w, vec_w, *sends = spread(mine_w, vec_w, came, part_high, (1, None, None), 2)
+    came_w = [
+        swap(s, m) for s, m in zip(sends, (2 * BIT_Z, BIT_X, 2 * BIT_Z | BIT_X))
+    ]
+    grad_frames = input_grads(4, 2, frames, grad_hidden, table, weights, done, [grad_frames])
+    came_w, grad_frames = together((came_w, grad_frames))
     down_grad, up_grad, out_grad, query_grad, key_grad, value_grad, *vectors = finish(
         mine, vec, mine_w, vec_w, came_z, came_w, ff, ow
     )

time: 224 us -> 188 us (0.84); the launches traced: 227 us -> 187 us
  starting transfers between devices: 54.5 us -> 35.3 us
  waiting for transfers between devices: 26.1 us -> 15.3 us
  local copies, waits for them, and re-layouts: 7.82 us -> 0.87 us
    ppermute x30, starting transfers between devices: 54.5 us -> 35.3 us  [swap(): lax.ppermute(values, ('dp', 'head'), [(i, i ^ mask) for i in range(device...]
    ppermute x30, waiting for transfers between devices: 26.1 us -> 15.3 us  [swap(): lax.ppermute(values, ('dp', 'head'), [(i, i ^ mask) for i in range(device...]
    unnamed x29 -> x19, local copies, waits for them, and re-layouts: 7.76 us -> 0.81 us
    pallas_call x3, Pallas kernels: 58.4 us -> 55.4 us  [attend_backward_fast(): pl.pallas_call(functools.partial(backward_kernel, first), grid=(pairs, ro...]
    pallas_call x1, Pallas kernels: 35.9 us -> 33.2 us  [middle(): pl.pallas_call(functools.partial(middle_kernel, masks), grid=(rows // til...]
    pallas_call x1 -> x2, Pallas kernels: 4.66 us -> 5.84 us  [input_grads(): pl.pallas_call(functools.partial(input_grad_kernel, first), grid=(tiles,)...]
  transfers between devices with their start and end apart: 30 -> 30, of which waited for: 16 -> 8; matrix products, arithmetic and copies ran while one was open for 0% -> 0% of each run, Pallas kernels for 43% -> 52%
where the time goes in v1:
time: 188 us; the launch traced here: 187 us
  Pallas kernels  135 us (72%)
  starting transfers between devices  35.3 us (19%)
  waiting for transfers between devices  15.3 us (8%)
    pallas_call x3, Pallas kernels, attend_backward_fast(): pl.pallas_call(functools.partial(backward_kernel, first), grid=(pairs, ro...  55.4 us
    ppermute x30, starting transfers between devices, swap(): lax.ppermute(values, ('dp', 'head'), [(i, i ^ mask) for i in range(device...  35.3 us
    pallas_call x2, Pallas kernels, attend_forward_fast(): pl.pallas_call(functools.partial(forward_kernel, side_at), grid=(pairs, r...  33.9 us
    pallas_call x1, Pallas kernels, middle(): pl.pallas_call(functools.partial(middle_kernel, masks), grid=(rows // til...  33.2 us
    ppermute x30, waiting for transfers between devices, swap(): lax.ppermute(values, ('dp', 'head'), [(i, i ^ mask) for i in range(device...  15.3 us
    pallas_call x2, Pallas kernels, input_grads(): pl.pallas_call(functools.partial(input_grad_kernel, first), grid=(tiles,)...  5.84 us
  transfers between devices with their start and end apart: 30, of which 8 were waited for; matrix products, arithmetic and copies ran while one was open for 0% of the time, Pallas kernels for 52%

profile of v1, /device:TPU:0, one launch (start us, length us, event | category | flops | bytes accessed | tf_op | source)
XLA Modules:
  0.0 187.3 jit_solution(15251395124105830672)
XLA Ops:
  0.7 0.0 copy-start.2
  0.7 2.0 %pack.1 = (bf16[1,96,256]{2,1,0:T(8,128)(2,1)}, bf16[288,256]{1,0:T(8,128)(2,1)}, f32[16,512]{1,0:T(8,128)}) custom-call(s32[32]{0:T(128)} %live_ref.1, s32[32]{0:T(128)} %language_ref.1, s32[32]{0:T(128)} %task_ref.1, bf16[32,256]{1,0:T(8,128)(2,1)} %query_ref.1, bf16[32,256]{1,0:T(8,128)(2,1)} %key_ref.1, bf16[32,256]{1,0:T(8,128)(2,1)} %value_ref.1, ...), custom_call_target="tpu_custom_call" | custom-call | flops 3000000000 | bytes 1048576 | tf_op jit(solution)/shard_map/pack/pallas_call | solution.py:390
  2.7 4.0 %collective-permute-start = (bf16[1,96,256]{2,1,0:T(8,128)(2,1)}, bf16[1,96,256]{2,1,0:T(8,128)(2,1)S(1)}, u32[]{:S(2)}, u32[]{:S(2)}) collective-permute-start(bf16[1,96,256]{2,1,0:T(8,128)(2,1)} %get-tuple-element.139), channel_id=1, source_target_pairs={{0,16},{1,17},{2,18},{3,19},{4,20},{5,21},{6,22},{7,23},{8,24},{9,... | collective-permute-start | bytes 147464 | tf_op jit(solution)/shard_map/ppermute | solution.py:929
  6.7 0.8 copy-done.4
  7.5 2.1 %first_norm.1 = (bf16[1536,512]{1,0:T(8,128)(2,1)S(1)}, bf16[512,1536]{1,0:T(8,128)(2,1)S(1)}) custom-call(bf16[1500,512]{1,0:T(8,128)(2,1)S(1)} %copy-done.2, f32[16,512]{1,0:T(8,128)S(1)} %copy-done.4), custom_call_target="tpu_custom_call" | custom-call | flops 4000000000 | bytes 1048576 | tf_op jit(solution)/shard_map/first_norm/pallas_call | solution.py:430
  9.6 0.0 copy-start.5
  9.6 0.0 collective-permute-done
  9.7 2.4 %collective-permute-start.4 = (bf16[1,288,256]{2,1,0:T(8,128)(2,1)S(1)}, bf16[1,288,256]{2,1,0:T(8,128)(2,1)S(1)}, u32[]{:S(2)}, u32[]{:S(2)}) collective-permute-start(bf16[1,288,256]{2,1,0:T(8,128)(2,1)S(1)} %bitcast.25), channel_id=1, source_target_pairs={{0,16},{1,17},{2,18},{3,19},{4,20},{5,21},{6,22},{7,23},{8,24},{9,... | collective-permute-start | bytes 442376 | tf_op jit(solution)/shard_map/ppermute | solution.py:929
  12.0 1.9 %collective-permute-start.1 = (bf16[2,96,256]{2,1,0:T(8,128)(2,1)S(1)}, bf16[2,96,256]{2,1,0:T(8,128)(2,1)S(1)}, u32[]{:S(2)}, u32[]{:S(2)}) collective-permute-start(bf16[2,96,256]{2,1,0:T(8,128)(2,1)S(1)} %pad_maximum_fusion.3), channel_id=1, source_target_pairs={{0,8},{1,9},{2,10},{3,11},{4,12},{5,13},{6,14},{7,15},{8,0},{9,1},... | collective-permute-start | bytes 294920 | tf_op jit(solution)/shard_map/ppermute | solution.py:929
  14.0 3.6 %collective-permute-done.1 = bf16[2,96,256]{2,1,0:T(8,128)(2,1)S(1)} collective-permute-done((bf16[2,96,256]{2,1,0:T(8,128)(2,1)S(1)}, bf16[2,96,256]{2,1,0:T(8,128)(2,1)S(1)}, u32[]{:S(2)}, u32[]{:S(2)}) %collective-permute-start.1) | collective-permute-done | bytes 98336 | tf_op jit(solution)/shard_map/ppermute | solution.py:929
  17.6 1.6 collective-permute-start.2
  19.2 0.0 collective-permute-done.4
  19.3 1.1 collective-permute-start.5
  20.4 3.0 %collective-permute-done.2 = bf16[4,96,256]{2,1,0:T(8,128)(2,1)S(1)} collective-permute-done((bf16[4,96,256]{2,1,0:T(8,128)(2,1)S(1)}, bf16[4,96,256]{2,1,0:T(8,128)(2,1)S(1)}, u32[]{:S(2)}, u32[]{:S(2)}) %collective-permute-start.2) | collective-permute-done | bytes 196640 | tf_op jit(solution)/shard_map/ppermute | solution.py:929
  23.4 0.1 collective-permute-start.6
  23.5 1.6 collective-permute-start.3
  25.0 1.5 collective-permute-done.5
  26.6 0.1 pad_maximum_fusion.refs_0_
  26.6 0.0 collective-permute-done.6.far_ref
  26.6 1.6 collective-permute-start.7
  28.2 1.5 collective-permute-start.8
  29.7 16.9 %attend_forward.2 = (bf16[1536,512]{1,0:T(8,128)(2,1)S(1)}, bf16[1536,512]{1,0:T(8,128)(2,1)S(1)}, bf16[1536,512]{1,0:T(8,128)(2,1)S(1)}, bf16[8,1536,1536]{2,1,...) custom-call(bf16[1536,512]{1,0:T(8,128)(2,1)S(1)} %get-tuple-element, ...), custom_call_target="tpu_custom_call" | custom-call | flops 15000000512 | bytes 1048576 | tf_op jit(solution)/shard_map/attend_forward/pallas_call | solution.py:556
  46.6 0.0 collective-permute-done.3.near_ref
  46.6 0.0 collective-permute-done.7.refs_1_
  46.6 1.0 collective-permute-done.8.refs_2_
  47.6 0.5 collective-permute-start.11
  48.2 1.5 collective-permute-start.9
  49.6 0.0 collective-permute-start.12
  49.7 0.5 collective-permute-start.13
  50.2 16.9 %attend_forward.3 = (bf16[1536,512]{1,0:T(8,128)(2,1)S(1)}, bf16[1536,512]{1,0:T(8,128)(2,1)S(1)}, bf16[1536,512]{1,0:T(8,128)(2,1)S(1)}, bf16[8,1536,1536]{2,1,...) custom-call(bf16[1536,512]{1,0:T(8,128)(2,1)S(1)} %get-tuple-element, ...), custom_call_target="tpu_custom_call", output_to_operand_aliasing={{0}: (4, {}), {1}: (5, {}), {2}: (6, {}), {3}: (7, {}), {4}... | custom-call | flops 15000000512 | bytes 1048576 | tf_op jit(solution)/shard_map/attend_forward/pallas_call | solution.py:556
  67.1 0.0 collective-permute-done.9.refs_3_
  67.1 0.1 collective-permute-start.14
  67.3 1.9 %collective-permute-done.14.refs_7_ = bf16[4,288,256]{2,1,0:T(8,128)(2,1)S(1)} collective-permute-done((bf16[4,288,256]{2,1,0:T(8,128)(2,1)S(1)}, bf16[4,288,256]{2,1,0:T(8,128)(2,1)S(1)}, u32[]{:S(2)}, u32[]{:S(2)}) %collective-permute-start.14) | collective-permute-done | bytes 589856 | tf_op jit(solution)/shard_map/ppermute | solution.py:929
  69.2 33.2 %middle.1 = (bf16[1500,512]{1,0:T(8,128)(2,1)}, bf16[1536,512]{1,0:T(8,128)(2,1)}, f32[1536,512]{1,0:T(8,128)}, bf16[4640,256]{1,0:T(8,128)(2,1)S(1)}, bf16[4608...) custom-call(bf16[1536,512]{1,0:T(8,128)(2,1)} %get-tuple-element.162.c_ref, bf16[1500,512]{1,0:T(8,128)(2,1)} %x_ref.7, ...), custom_call_target="tpu_custom_call" | custom-call | flops 38000001024 | bytes 1048576 | tf_op jit(solution)/shard_map/middle/pallas_call | solution.py:835
  102.4 0.1 collective-permute-start.15
  102.5 14.4 %attend_backward.3 = (bf16[1536,512]{1,0:T(8,128)(2,1)S(1)}, bf16[1536,512]{1,0:T(8,128)(2,1)S(1)}, bf16[1536,512]{1,0:T(8,128)(2,1)S(1)}, bf16[2,3,512,256]{3,2,1,0:T(8,128)(2,1)S(1)}, f32[8,512]{1,0:T(8,128)S(1)}) custom-call(bf16[1536,512]{1,0:T(8,128)(2,1)S(1)} %get-tuple-element.166.q_ref, bf16[1536,512]{1,0:T(8,128)(2,1)S(1)} %get-tuple-element.167.k_ref, ...), custom_call_target="tpu_custom_call" | custom-call | flops 14000000000 | bytes 1048576 | tf_op jit(solution)/shard_map/attend_backward/pallas_call | solution.py:675
  117.0 0.6 spread.4
  117.6 0.8 collective-permute-start.16
  118.4 1.5 collective-permute-start.17
  119.9 1.2 collective-permute-start.18
  121.1 26.6 %attend_backward.4 = (bf16[1536,512]{1,0:T(8,128)(2,1)S(1)}, bf16[1536,512]{1,0:T(8,128)(2,1)S(1)}, bf16[1536,512]{1,0:T(8,128)(2,1)S(1)}, bf16[2,3,512,256]{3,2,1,0:T(8,128)(2,1)S(1)}, f32[8,512]{1,0:T(8,128)S(1)}) custom-call(bf16[1536,512]{1,0:T(8,128)(2,1)S(1)} %get-tuple-element.166., ...), custom_call_target="tpu_custom_call", output_to_operand_aliasing={{0}: (11, {}), {1}: (12, {}), {2}: (13, {}), {3}: (14, {})} | custom-call | flops 28000000000 | bytes 1048576 | tf_op jit(solution)/shard_map/attend_backward/pallas_call | solution.py:675
  147.8 0.1 slice_bitcast_fusion
  147.9 0.3 spread.5
  148.2 0.8 collective-permute-start.22
  149.0 1.0 collective-permute-start.19
  150.0 1.5 collective-permute-start.20
  151.5 1.9 collective-permute-start.21
  153.3 14.3 %attend_backward.5 = (bf16[1536,512]{1,0:T(8,128)(2,1)S(1)}, bf16[1536,512]{1,0:T(8,128)(2,1)S(1)}, bf16[1536,512]{1,0:T(8,128)(2,1)S(1)}, bf16[2,3,512,256]{3,2,1,0:T(8,128)(2,1)S(1)}, f32[8,512]{1,0:T(8,128)S(1)}) custom-call(bf16[1536,512]{1,0:T(8,128)(2,1)S(1)} %get-tuple-element.166., ...), custom_call_target="tpu_custom_call", output_to_operand_aliasing={{0}: (11, {}), {1}: (12, {}), {2}: (13, {}), {3}: (14, {})} | custom-call | flops 14000000000 | bytes 1048576 | tf_op jit(solution)/shard_map/attend_backward/pallas_call | solution.py:675
  167.7 0.3 gather_grads.1
  168.1 0.1 collective-permute-start.23
  168.1 1.7 collective-permute-done.23.refs_0_
  169.9 0.1 spread.6
  170.0 0.4 collective-permute-start.24
  170.4 1.5 collective-permute-start.25
  172.0 1.6 collective-permute-start.26
  173.5 3.7 %input_grads.2.refs_0_ = bf16[1500,512]{1,0:T(8,128)(2,1)} custom-call(bf16[1500,512]{1,0:T(8,128)(2,1)S(1)} %copy-done.3, f32[1536,512]{1,0:T(8,128)S(1)} %copy-done.1, f32[16,512]{1,0:T(8,128)S(1)} %copy-done.5, bf16[3,512,512]{2,1,0:T(8,128)(2,1)S(1)} %copy-done, bf16[1536,512]{1,0:T(8,128)(2,1)S(1)} %get-tuple-element.225.dq_ref, ...), custom_call_target="tpu_custom_call" | custom-call | flops 4000000000 | bytes 1048576 | tf_op jit(solution)/shard_map/input_grads/pallas_call | solution.py:1063
  177.2 1.1 collective-permute-done.26.refs_2_
  178.3 0.1 spread.7
  178.4 1.4 collective-permute-start.27
  179.8 1.1 collective-permute-start.28
  180.9 1.9 %collective-permute-start.29 = (bf16[16,256]{1,0:T(8,128)(2,1)S(1)}, bf16[16,256]{1,0:T(8,128)(2,1)S(1)}, u32[]{:S(2)}, u32[]{:S(2)}) collective-permute-start(bf16[16,256]{1,0:T(8,128)(2,1)S(1)} %get-tuple-element.233), channel_id=1, source_target_pairs={{0,17},{1,16},{2,19},{3,18},{4,21},{5,20},{6,23},{7,22},{8,25},{9,... | collective-permute-start | bytes 24584 | tf_op jit(solution)/shard_map/ppermute | solution.py:929
  182.8 2.2 %input_grads.3 = bf16[1500,512]{1,0:T(8,128)(2,1)} custom-call(bf16[1500,512]{1,0:T(8,128)(2,1)S(1)} %copy-done.3, f32[1536,512]{1,0:T(8,128)S(1)} %copy-done.1, f32[16,512]{1,0:T(8,128)S(1)} %copy-done.5, bf16[3,512,512]{2,1,0:T(8,128)(2,1)S(1)} %copy-done, bf16[1536,512]{1,0:T(8,128)(2,1)S(1)} %get-tuple-element.225.dq_ref, ...), custom_call_target="tpu_custom_call", output_to_operand_aliasing={{}: (7, {})} | custom-call | flops 2000000000 | bytes 1048576 | tf_op jit(solution)/shard_map/input_grads/pallas_call | solution.py:1063
  185.0 1.3 collective-permute-done.29.refs_5_
  186.3 0.8 finish.1
  (38 shorter events, 0.2 us)
Async XLA Ops:
  0.7 6.0 %copy-start.2 = (bf16[1500,512]{1,0:T(8,128)(2,1)S(1)}, bf16[1500,512]{1,0:T(8,128)(2,1)}, u32[]{:S(2)}) copy-start(bf16[1500,512]{1,0:T(8,128)(2,1)} %x_ref.7) | copy-start | bytes 4608004
  2.7 7.0 %collective-permute-start = (bf16[1,96,256]{2,1,0:T(8,128)(2,1)}, bf16[1,96,256]{2,1,0:T(8,128)(2,1)S(1)}, u32[]{:S(2)}, u32[]{:S(2)}) collective-permute-start(bf16[1,96,256]{2,1,0:T(8,128)(2,1)} %get-tuple-element.139), channel_id=1, source_target_pairs={{0,16},{1,17},{2,18},{3,19},{4,20},{5,21},{6,22},{7,23},{8,24},{9,... | collective-permute-start | bytes 147464 | tf_op jit(solution)/shard_map/ppermute | solution.py:929
  6.7 0.8 copy-start.4
  7.5 2.1 %copy-start.6 = (bf16[1,96,256]{2,1,0:T(8,128)(2,1)S(1)}, bf16[1,96,256]{2,1,0:T(8,128)(2,1)}, u32[]{:S(2)}) copy-start(bf16[1,96,256]{2,1,0:T(8,128)(2,1)} %get-tuple-element.139) | copy-start | bytes 147460
  7.5 2.2 %copy-start.7 = (bf16[288,256]{1,0:T(8,128)(2,1)S(1)}, bf16[288,256]{1,0:T(8,128)(2,1)}, u32[]{:S(2)}) copy-start(bf16[288,256]{1,0:T(8,128)(2,1)} %get-tuple-element.144) | copy-start | bytes 442372
  9.6 20.1 %copy-start.5 = (f32[16,512]{1,0:T(8,128)S(1)}, f32[16,512]{1,0:T(8,128)}, u32[]{:S(2)}) copy-start(f32[16,512]{1,0:T(8,128)} %get-tuple-element.140.table_ref) | copy-start | bytes 98308
  9.7 9.6 %collective-permute-start.4 = (bf16[1,288,256]{2,1,0:T(8,128)(2,1)S(1)}, bf16[1,288,256]{2,1,0:T(8,128)(2,1)S(1)}, u32[]{:S(2)}, u32[]{:S(2)}) collective-permute-start(bf16[1,288,256]{2,1,0:T(8,128)(2,1)S(1)} %bitcast.25), channel_id=1, source_target_pairs={{0,16},{1,17},{2,18},{3,19},{4,20},{5,21},{6,22},{7,23},{8,24},{9,... | collective-permute-start | bytes 442376 | tf_op jit(solution)/shard_map/ppermute | solution.py:929
  12.0 5.6 %collective-permute-start.1 = (bf16[2,96,256]{2,1,0:T(8,128)(2,1)S(1)}, bf16[2,96,256]{2,1,0:T(8,128)(2,1)S(1)}, u32[]{:S(2)}, u32[]{:S(2)}) collective-permute-start(bf16[2,96,256]{2,1,0:T(8,128)(2,1)S(1)} %pad_maximum_fusion.3), channel_id=1, source_target_pairs={{0,8},{1,9},{2,10},{3,11},{4,12},{5,13},{6,14},{7,15},{8,0},{9,1},... | collective-permute-start | bytes 294920 | tf_op jit(solution)/shard_map/ppermute | solution.py:929
  17.6 5.7 %collective-permute-start.2 = (bf16[4,96,256]{2,1,0:T(8,128)(2,1)S(1)}, bf16[4,96,256]{2,1,0:T(8,128)(2,1)S(1)}, u32[]{:S(2)}, u32[]{:S(2)}) collective-permute-start(bf16[4,96,256]{2,1,0:T(8,128)(2,1)S(1)} %pad_maximum_fusion.2), channel_id=1, source_target_pairs={{0,4},{1,5},{2,6},{3,7},{4,0},{5,1},{6,2},{7,3},{8,12},{9,13},{10,... | collective-permute-start | bytes 589832 | tf_op jit(solution)/shard_map/ppermute | solution.py:929
  19.3 7.3 %collective-permute-start.5 = (bf16[2,288,256]{2,1,0:T(8,128)(2,1)S(1)}, bf16[2,288,256]{2,1,0:T(8,128)(2,1)S(1)}, u32[]{:S(2)}, u32[]{:S(2)}) collective-permute-start(bf16[2,288,256]{2,1,0:T(8,128)(2,1)S(1)} %pad_maximum_fusion.1), channel_id=1, source_target_pairs={{0,8},{1,9},{2,10},{3,11},{4,12},{5,13},{6,14},{7,15},{8,0},{9,1},... | collective-permute-start | bytes 884744 | tf_op jit(solution)/shard_map/ppermute | solution.py:929
  23.4 3.2 %collective-permute-start.6 = (bf16[8,96,256]{2,1,0:T(8,128)(2,1)S(1)}, bf16[8,96,256]{2,1,0:T(8,128)(2,1)S(1)}, u32[]{:S(2)}, u32[]{:S(2)}) collective-permute-start(bf16[8,96,256]{2,1,0:T(8,128)(2,1)S(1)} %constant_dynamic-update-slice_fusion.near_ref), channel_id=1, source_target_pairs={{0,2},{1,3},{2,0},{3,1},{4,6},{5,7},{6,4},{7,5},{8,10},{9,11},{10,... | collective-permute-start | bytes 1179656 | tf_op jit(solution)/shard_map/ppermute | solution.py:929
  23.5 23.2 %collective-permute-start.3 = (bf16[8,96,256]{2,1,0:T(8,128)(2,1)S(1)}, bf16[8,96,256]{2,1,0:T(8,128)(2,1)S(1)}, u32[]{:S(2)}, u32[]{:S(2)}) collective-permute-start(bf16[8,96,256]{2,1,0:T(8,128)(2,1)S(1)} %constant_dynamic-update-slice_fusion.near_ref), channel_id=1, source_target_pairs={{0,1},{1,0},{2,3},{3,2},{4,5},{5,4},{6,7},{7,6},{8,9},{9,8},{10,11... | collective-permute-start | bytes 1179656 | tf_op jit(solution)/shard_map/ppermute | solution.py:929
  26.6 20.0 %collective-permute-start.7 = (bf16[4,288,256]{2,1,0:T(8,128)(2,1)S(1)}, bf16[4,288,256]{2,1,0:T(8,128)(2,1)S(1)}, u32[]{:S(2)}, u32[]{:S(2)}) collective-permute-start(bf16[4,288,256]{2,1,0:T(8,128)(2,1)S(1)} %pad_maximum_fusion.refs_0_), channel_id=1, source_target_pairs={{0,4},{1,5},{2,6},{3,7},{4,0},{5,1},{6,2},{7,3},{8,12},{9,13},{10,... | collective-permute-start | bytes 1769480 | tf_op jit(solution)/shard_map/ppermute | solution.py:929
  28.2 19.4 %collective-permute-start.8 = (bf16[4,288,256]{2,1,0:T(8,128)(2,1)S(1)}, bf16[4,288,256]{2,1,0:T(8,128)(2,1)S(1)}, u32[]{:S(2)}, u32[]{:S(2)}) collective-permute-start(bf16[4,288,256]{2,1,0:T(8,128)(2,1)S(1)} %pad_maximum_fusion.refs_0_), channel_id=1, source_target_pairs={{0,1},{1,0},{2,3},{3,2},{4,5},{5,4},{6,7},{7,6},{8,9},{9,8},{10,11... | collective-permute-start | bytes 1769480 | tf_op jit(solution)/shard_map/ppermute | solution.py:929
  47.6 2.5 %collective-permute-start.10 = (bf16[8,96,256]{2,1,0:T(8,128)(2,1)S(1)}, bf16[8,96,256]{2,1,0:T(8,128)(2,1)S(1)}, u32[]{:S(2)}, u32[]{:S(2)}) collective-permute-start(bf16[8,96,256]{2,1,0:T(8,128)(2,1)S(1)} %collective-permute-done.3.near_ref), channel_id=1, source_target_pairs={{0,2},{1,3},{2,0},{3,1},{4,6},{5,7},{6,4},{7,5},{8,10},{9,11},{10,... | collective-permute-start | bytes 1179656 | tf_op jit(solution)/shard_map/ppermute | solution.py:929
  47.6 19.6 %collective-permute-start.11 = (bf16[4,288,256]{2,1,0:T(8,128)(2,1)S(1)}, bf16[4,288,256]{2,1,0:T(8,128)(2,1)S(1)}, u32[]{:S(2)}, u32[]{:S(2)}) collective-permute-start(bf16[4,288,256]{2,1,0:T(8,128)(2,1)S(1)} %pad_maximum_fusion.refs_0_), channel_id=1, source_target_pairs={{0,2},{1,3},{2,0},{3,1},{4,6},{5,7},{6,4},{7,5},{8,10},{9,11},{10,... | collective-permute-start | bytes 1769480 | tf_op jit(solution)/shard_map/ppermute | solution.py:929
  48.2 18.9 %collective-permute-start.9 = (bf16[4,288,256]{2,1,0:T(8,128)(2,1)S(1)}, bf16[4,288,256]{2,1,0:T(8,128)(2,1)S(1)}, u32[]{:S(2)}, u32[]{:S(2)}) collective-permute-start(bf16[4,288,256]{2,1,0:T(8,128)(2,1)S(1)} %collective-permute-done.7.refs_1_), channel_id=1, source_target_pairs={{0,1},{1,0},{2,3},{3,2},{4,5},{5,4},{6,7},{7,6},{8,9},{9,8},{10,11... | collective-permute-start | bytes 1769480 | tf_op jit(solution)/shard_map/ppermute | solution.py:929
  49.6 17.6 %collective-permute-start.12 = (bf16[4,288,256]{2,1,0:T(8,128)(2,1)S(1)}, bf16[4,288,256]{2,1,0:T(8,128)(2,1)S(1)}, u32[]{:S(2)}, u32[]{:S(2)}) collective-permute-start(bf16[4,288,256]{2,1,0:T(8,128)(2,1)S(1)} %collective-permute-done.7.refs_1_), channel_id=1, source_target_pairs={{0,2},{1,3},{2,0},{3,1},{4,6},{5,7},{6,4},{7,5},{8,10},{9,11},{10,... | collective-permute-start | bytes 1769480 | tf_op jit(solution)/shard_map/ppermute | solution.py:929
  49.7 17.6 %collective-permute-start.13 = (bf16[4,288,256]{2,1,0:T(8,128)(2,1)S(1)}, bf16[4,288,256]{2,1,0:T(8,128)(2,1)S(1)}, u32[]{:S(2)}, u32[]{:S(2)}) collective-permute-start(bf16[4,288,256]{2,1,0:T(8,128)(2,1)S(1)} %collective-permute-done.8.refs_2_), channel_id=1, source_target_pairs={{0,2},{1,3},{2,0},{3,1},{4,6},{5,7},{6,4},{7,5},{8,10},{9,11},{10,... | collective-permute-start | bytes 1769480 | tf_op jit(solution)/shard_map/ppermute | solution.py:929
  67.1 2.1 %collective-permute-start.14 = (bf16[4,288,256]{2,1,0:T(8,128)(2,1)S(1)}, bf16[4,288,256]{2,1,0:T(8,128)(2,1)S(1)}, u32[]{:S(2)}, u32[]{:S(2)}) collective-permute-start(bf16[4,288,256]{2,1,0:T(8,128)(2,1)S(1)} %collective-permute-done.9.refs_3_), channel_id=1, source_target_pairs={{0,2},{1,3},{2,0},{3,1},{4,6},{5,7},{6,4},{7,5},{8,10},{9,11},{10,... | collective-permute-start | bytes 1769480 | tf_op jit(solution)/shard_map/ppermute | solution.py:929
  102.4 14.6 %collective-permute-start.15 = (bf16[4640,256]{1,0:T(8,128)(2,1)S(1)}, bf16[4640,256]{1,0:T(8,128)(2,1)S(1)}, u32[]{:S(2)}, u32[]{:S(2)}) collective-permute-start(bf16[4640,256]{1,0:T(8,128)(2,1)S(1)} %get-tuple-element.174), channel_id=1, source_target_pairs={{0,2},{1,3},{2,0},{3,1},{4,6},{5,7},{6,4},{7,5},{8,10},{9,11},{10,... | collective-permute-start | bytes 7127048 | tf_op jit(solution)/shard_map/ppermute | solution.py:929
  117.6 30.3 %collective-permute-start.16 = (bf16[1184,256]{1,0:T(8,128)(2,1)S(1)}, bf16[1184,256]{1,0:T(8,128)(2,1)S(1)}, u32[]{:S(2)}, u32[]{:S(2)}) collective-permute-start(bf16[1184,256]{1,0:T(8,128)(2,1)S(1)} %get-tuple-element.183), channel_id=1, source_target_pairs={{0,1},{1,0},{2,3},{3,2},{4,5},{5,4},{6,7},{7,6},{8,9},{9,8},{10,11... | collective-permute-start | bytes 1818632 | tf_op jit(solution)/shard_map/ppermute | solution.py:929
  118.4 29.5 %collective-permute-start.17 = (bf16[1184,256]{1,0:T(8,128)(2,1)S(1)}, bf16[1184,256]{1,0:T(8,128)(2,1)S(1)}, u32[]{:S(2)}, u32[]{:S(2)}) collective-permute-start(bf16[1184,256]{1,0:T(8,128)(2,1)S(1)} %get-tuple-element.184), channel_id=1, source_target_pairs={{0,4},{1,5},{2,6},{3,7},{4,0},{5,1},{6,2},{7,3},{8,12},{9,13},{10,... | collective-permute-start | bytes 1818632 | tf_op jit(solution)/shard_map/ppermute | solution.py:929
  119.9 28.0 %collective-permute-start.18 = (bf16[1184,256]{1,0:T(8,128)(2,1)S(1)}, bf16[1184,256]{1,0:T(8,128)(2,1)S(1)}, u32[]{:S(2)}, u32[]{:S(2)}) collective-permute-start(bf16[1184,256]{1,0:T(8,128)(2,1)S(1)} %get-tuple-element.185), channel_id=1, source_target_pairs={{0,5},{1,4},{2,7},{3,6},{4,1},{5,0},{6,3},{7,2},{8,13},{9,12},{10,... | collective-permute-start | bytes 1818632 | tf_op jit(solution)/shard_map/ppermute | solution.py:929
  148.2 19.6 %collective-permute-start.22 = (bf16[3,512,256]{2,1,0:T(8,128)(2,1)S(1)}, bf16[3,512,256]{2,1,0:T(8,128)(2,1)S(1)}, u32[]{:S(2)}, u32[]{:S(2)}) collective-permute-start(bf16[3,512,256]{2,1,0:T(8,128)(2,1)S(1)} %slice_bitcast_fusion), channel_id=1, source_target_pairs={{0,1},{1,0},{2,3},{3,2},{4,5},{5,4},{6,7},{7,6},{8,9},{9,8},{10,11... | collective-permute-start | bytes 2359304 | tf_op jit(solution)/shard_map/ppermute | solution.py:929
  149.0 18.7 %collective-permute-start.19 = (bf16[320,256]{1,0:T(8,128)(2,1)S(1)}, bf16[320,256]{1,0:T(8,128)(2,1)S(1)}, u32[]{:S(2)}, u32[]{:S(2)}) collective-permute-start(bf16[320,256]{1,0:T(8,128)(2,1)S(1)} %get-tuple-element.209), channel_id=1, source_target_pairs={{0,8},{1,9},{2,10},{3,11},{4,12},{5,13},{6,14},{7,15},{8,0},{9,1},... | collective-permute-start | bytes 491528 | tf_op jit(solution)/shard_map/ppermute | solution.py:929
  150.0 17.7 %collective-permute-start.20 = (bf16[320,256]{1,0:T(8,128)(2,1)S(1)}, bf16[320,256]{1,0:T(8,128)(2,1)S(1)}, u32[]{:S(2)}, u32[]{:S(2)}) collective-permute-start(bf16[320,256]{1,0:T(8,128)(2,1)S(1)} %get-tuple-element.210), channel_id=1, source_target_pairs={{0,16},{1,17},{2,18},{3,19},{4,20},{5,21},{6,22},{7,23},{8,24},{9,... | collective-permute-start | bytes 491528 | tf_op jit(solution)/shard_map/ppermute | solution.py:929
  151.5 16.2 %collective-permute-start.21 = (bf16[320,256]{1,0:T(8,128)(2,1)S(1)}, bf16[320,256]{1,0:T(8,128)(2,1)S(1)}, u32[]{:S(2)}, u32[]{:S(2)}) collective-permute-start(bf16[320,256]{1,0:T(8,128)(2,1)S(1)} %get-tuple-element.211), channel_id=1, source_target_pairs={{0,24},{1,25},{2,26},{3,27},{4,28},{5,29},{6,30},{7,31},{8,16},{9,... | collective-permute-start | bytes 491528 | tf_op jit(solution)/shard_map/ppermute | solution.py:929
  168.1 1.8 collective-permute-start.23
  169.9 3.7 %copy-start = (bf16[3,512,512]{2,1,0:T(8,128)(2,1)S(1)}, bf16[3,512,512]{2,1,0:T(8,128)(2,1)}, u32[]{:S(2)}) copy-start(bf16[3,512,512]{2,1,0:T(8,128)(2,1)} %get-tuple-element.188.w_ref) | copy-start | bytes 4718596
  169.9 3.7 %copy-start.1 = (f32[1536,512]{1,0:T(8,128)S(1)}, f32[1536,512]{1,0:T(8,128)}, u32[]{:S(2)}) copy-start(f32[1536,512]{1,0:T(8,128)} %get-tuple-element.224.gh_ref) | copy-start | bytes 9437188
  169.9 3.7 %copy-start.3 = (bf16[1500,512]{1,0:T(8,128)(2,1)S(1)}, bf16[1500,512]{1,0:T(8,128)(2,1)}, u32[]{:S(2)}) copy-start(bf16[1500,512]{1,0:T(8,128)(2,1)} %x_ref.7) | copy-start | bytes 4608004
  170.0 7.2 %collective-permute-start.24 = (bf16[208,256]{1,0:T(8,128)(2,1)S(1)}, bf16[208,256]{1,0:T(8,128)(2,1)S(1)}, u32[]{:S(2)}, u32[]{:S(2)}) collective-permute-start(bf16[208,256]{1,0:T(8,128)(2,1)S(1)} %get-tuple-element.221), channel_id=1, source_target_pairs={{0,8},{1,9},{2,10},{3,11},{4,12},{5,13},{6,14},{7,15},{8,0},{9,1},... | collective-permute-start | bytes 319496 | tf_op jit(solution)/shard_map/ppermute | solution.py:929
  170.4 6.8 %collective-permute-start.25 = (bf16[208,256]{1,0:T(8,128)(2,1)S(1)}, bf16[208,256]{1,0:T(8,128)(2,1)S(1)}, u32[]{:S(2)}, u32[]{:S(2)}) collective-permute-start(bf16[208,256]{1,0:T(8,128)(2,1)S(1)} %get-tuple-element.222), channel_id=1, source_target_pairs={{0,4},{1,5},{2,6},{3,7},{4,0},{5,1},{6,2},{7,3},{8,12},{9,13},{10,... | collective-permute-start | bytes 319496 | tf_op jit(solution)/shard_map/ppermute | solution.py:929
  172.0 6.3 %collective-permute-start.26 = (bf16[208,256]{1,0:T(8,128)(2,1)S(1)}, bf16[208,256]{1,0:T(8,128)(2,1)S(1)}, u32[]{:S(2)}, u32[]{:S(2)}) collective-permute-start(bf16[208,256]{1,0:T(8,128)(2,1)S(1)} %get-tuple-element.223), channel_id=1, source_target_pairs={{0,12},{1,13},{2,14},{3,15},{4,8},{5,9},{6,10},{7,11},{8,4},{9,5},... | collective-permute-start | bytes 319496 | tf_op jit(solution)/shard_map/ppermute | solution.py:929
  178.4 8.0 %collective-permute-start.27 = (bf16[112,256]{1,0:T(8,128)(2,1)S(1)}, bf16[112,256]{1,0:T(8,128)(2,1)S(1)}, u32[]{:S(2)}, u32[]{:S(2)}) collective-permute-start(bf16[112,256]{1,0:T(8,128)(2,1)S(1)} %get-tuple-element.231), channel_id=1, source_target_pairs={{0,16},{1,17},{2,18},{3,19},{4,20},{5,21},{6,22},{7,23},{8,24},{9,... | collective-permute-start | bytes 172040 | tf_op jit(solution)/shard_map/ppermute | solution.py:929
  179.8 5.2 %collective-permute-start.28 = (bf16[16,256]{1,0:T(8,128)(2,1)S(1)}, bf16[16,256]{1,0:T(8,128)(2,1)S(1)}, u32[]{:S(2)}, u32[]{:S(2)}) collective-permute-start(bf16[16,256]{1,0:T(8,128)(2,1)S(1)} %get-tuple-element.232), channel_id=1, source_target_pairs={{0,1},{1,0},{2,3},{3,2},{4,5},{5,4},{6,7},{7,6},{8,9},{9,8},{10,11... | collective-permute-start | bytes 24584 | tf_op jit(solution)/shard_map/ppermute | solution.py:929
  180.9 5.4 %collective-permute-start.29 = (bf16[16,256]{1,0:T(8,128)(2,1)S(1)}, bf16[16,256]{1,0:T(8,128)(2,1)S(1)}, u32[]{:S(2)}, u32[]{:S(2)}) collective-permute-start(bf16[16,256]{1,0:T(8,128)(2,1)S(1)} %get-tuple-element.233), channel_id=1, source_target_pairs={{0,17},{1,16},{2,19},{3,18},{4,21},{5,20},{6,23},{7,22},{8,25},{9,... | collective-permute-start | bytes 24584 | tf_op jit(solution)/shard_map/ppermute | solution.py:929

commit v2 on v1

--- a/solution.py
+++ b/solution.py
@@ -1122,8 +1122,8 @@
     came = swap(pieces, 2 * BIT_Z)
     normed, normed_t = first_norm(frames, table)
     came, normed = together((came, normed))
-    big = after(big[None], came)
     pieces = doubled(pieces, came)
+    big = after(big[None], (pieces, normed_t))
     big = doubled(big, swap(big, 2 * BIT_Z))
     came = swap(pieces, BIT_Z)
     big = after(big, came)

time: 188 us -> 187 us (level)
  no operation moved by 1% of the time
where the time goes in v2:
time: 187 us
  Pallas kernels  135 us (72%)
  starting transfers between devices  34.1 us (18%)
  waiting for transfers between devices  15.9 us (9%)
    pallas_call x3, Pallas kernels, attend_backward_fast(): pl.pallas_call(functools.partial(backward_kernel, first), grid=(pairs, ro...  55.4 us
    ppermute x30, starting transfers between devices, swap(): lax.ppermute(values, ('dp', 'head'), [(i, i ^ mask) for i in range(device...  34.1 us
    pallas_call x2, Pallas kernels, attend_forward_fast(): pl.pallas_call(functools.partial(forward_kernel, side_at), grid=(pairs, r...  34 us
    pallas_call x1, Pallas kernels, middle(): pl.pallas_call(functools.partial(middle_kernel, masks), grid=(rows // til...  33.2 us
    ppermute x30, waiting for transfers between devices, swap(): lax.ppermute(values, ('dp', 'head'), [(i, i ^ mask) for i in range(device...  15.9 us
    pallas_call x2, Pallas kernels, input_grads(): pl.pallas_call(functools.partial(input_grad_kernel, first), grid=(tiles,)...  5.84 us
  transfers between devices with their start and end apart: 30, of which 8 were waited for; matrix products, arithmetic and copies ran while one was open for 0% of the time, Pallas kernels for 52%

profile of v2, /device:TPU:0, one launch (start us, length us, event | category | flops | bytes accessed | tf_op | source)
XLA Modules:
  0.0 187.0 jit_solution(6417256237406796844)
XLA Ops:
  0.7 0.0 copy-start.2
  0.7 2.0 %pack.1 = (bf16[1,96,256]{2,1,0:T(8,128)(2,1)}, bf16[288,256]{1,0:T(8,128)(2,1)}, f32[16,512]{1,0:T(8,128)}) custom-call(s32[32]{0:T(128)} %live_ref.1, s32[32]{0:T(128)} %language_ref.1, s32[32]{0:T(128)} %task_ref.1, bf16[32,256]{1,0:T(8,128)(2,1)} %query_ref.1, bf16[32,256]{1,0:T(8,128)(2,1)} %key_ref.1, bf16[32,256]{1,0:T(8,128)(2,1)} %value_ref.1, ...), custom_call_target="tpu_custom_call" | custom-call | flops 3000000000 | bytes 1048576 | tf_op jit(solution)/shard_map/pack/pallas_call | solution.py:390
  2.7 4.0 %collective-permute-start = (bf16[1,96,256]{2,1,0:T(8,128)(2,1)}, bf16[1,96,256]{2,1,0:T(8,128)(2,1)S(1)}, u32[]{:S(2)}, u32[]{:S(2)}) collective-permute-start(bf16[1,96,256]{2,1,0:T(8,128)(2,1)} %get-tuple-element.139), channel_id=1, source_target_pairs={{0,16},{1,17},{2,18},{3,19},{4,20},{5,21},{6,22},{7,23},{8,24},{9,... | collective-permute-start | bytes 147464 | tf_op jit(solution)/shard_map/ppermute | solution.py:929
  6.7 0.8 copy-done.4
  7.5 2.1 %first_norm.1 = (bf16[1536,512]{1,0:T(8,128)(2,1)S(1)}, bf16[512,1536]{1,0:T(8,128)(2,1)S(1)}) custom-call(bf16[1500,512]{1,0:T(8,128)(2,1)S(1)} %copy-done.2, f32[16,512]{1,0:T(8,128)S(1)} %copy-done.4), custom_call_target="tpu_custom_call" | custom-call | flops 4000000000 | bytes 1048576 | tf_op jit(solution)/shard_map/first_norm/pallas_call | solution.py:430
  9.6 0.0 copy-start.5
  9.7 1.6 collective-permute-start.1
  11.3 2.7 %collective-permute-start.4 = (bf16[1,288,256]{2,1,0:T(8,128)(2,1)S(1)}, bf16[1,288,256]{2,1,0:T(8,128)(2,1)S(1)}, u32[]{:S(2)}, u32[]{:S(2)}) collective-permute-start(bf16[1,288,256]{2,1,0:T(8,128)(2,1)S(1)} %bitcast.25), channel_id=1, source_target_pairs={{0,16},{1,17},{2,18},{3,19},{4,20},{5,21},{6,22},{7,23},{8,24},{9,... | collective-permute-start | bytes 442376 | tf_op jit(solution)/shard_map/ppermute | solution.py:929
  14.0 0.4 collective-permute-done.1
  14.4 1.6 collective-permute-start.2
  16.1 4.3 %collective-permute-done.4 = bf16[1,288,256]{2,1,0:T(8,128)(2,1)S(1)} collective-permute-done((bf16[1,288,256]{2,1,0:T(8,128)(2,1)S(1)}, bf16[1,288,256]{2,1,0:T(8,128)(2,1)S(1)}, u32[]{:S(2)}, u32[]{:S(2)}) %collective-permute-start.4) | collective-permute-done | bytes 147488 | tf_op jit(solution)/shard_map/ppermute | solution.py:929
  20.4 0.1 collective-permute-start.5
  20.5 0.1 collective-permute-start.6
  20.5 1.6 collective-permute-start.3
  22.1 7.0 %collective-permute-done.5 = bf16[2,288,256]{2,1,0:T(8,128)(2,1)S(1)} collective-permute-done((bf16[2,288,256]{2,1,0:T(8,128)(2,1)S(1)}, bf16[2,288,256]{2,1,0:T(8,128)(2,1)S(1)}, u32[]{:S(2)}, u32[]{:S(2)}) %collective-permute-start.5) | collective-permute-done | bytes 294944 | tf_op jit(solution)/shard_map/ppermute | solution.py:929
  29.1 0.1 pad_maximum_fusion.refs_0_
  29.2 0.0 collective-permute-done.6.far_ref
  29.2 1.6 collective-permute-start.7
  30.8 1.5 collective-permute-start.8
  32.3 17.0 %attend_forward.2 = (bf16[1536,512]{1,0:T(8,128)(2,1)S(1)}, bf16[1536,512]{1,0:T(8,128)(2,1)S(1)}, bf16[1536,512]{1,0:T(8,128)(2,1)S(1)}, bf16[8,1536,1536]{2,1,...) custom-call(bf16[1536,512]{1,0:T(8,128)(2,1)S(1)} %get-tuple-element, ...), custom_call_target="tpu_custom_call" | custom-call | flops 15000000512 | bytes 1048576 | tf_op jit(solution)/shard_map/attend_forward/pallas_call | solution.py:556
  49.2 0.0 collective-permute-done.3.near_ref
  49.2 0.0 collective-permute-done.7.refs_1_
  49.3 0.1 collective-permute-start.10
  49.3 0.5 collective-permute-start.11
  49.8 0.5 collective-permute-start.9
  50.4 0.0 collective-permute-start.12
  50.4 0.5 collective-permute-start.13
  50.9 0.2 collective-permute-done.10.far_ref
  51.0 17.0 %attend_forward.3 = (bf16[1536,512]{1,0:T(8,128)(2,1)S(1)}, bf16[1536,512]{1,0:T(8,128)(2,1)S(1)}, bf16[1536,512]{1,0:T(8,128)(2,1)S(1)}, bf16[8,1536,1536]{2,1,...) custom-call(bf16[1536,512]{1,0:T(8,128)(2,1)S(1)} %get-tuple-element, ...), custom_call_target="tpu_custom_call", output_to_operand_aliasing={{0}: (4, {}), {1}: (5, {}), {2}: (6, {}), {3}: (7, {}), {4}... | custom-call | flops 15000000512 | bytes 1048576 | tf_op jit(solution)/shard_map/attend_forward/pallas_call | solution.py:556
  68.1 0.2 collective-permute-start.14
  68.3 0.0 collective-permute-done.11.refs_4_
  68.3 0.0 collective-permute-done.12.refs_5_
  68.3 1.9 collective-permute-done.14.refs_7_
  70.2 33.2 %middle.1 = (bf16[1500,512]{1,0:T(8,128)(2,1)}, bf16[1536,512]{1,0:T(8,128)(2,1)}, f32[1536,512]{1,0:T(8,128)}, bf16[4640,256]{1,0:T(8,128)(2,1)S(1)}, bf16[4608...) custom-call(bf16[1536,512]{1,0:T(8,128)(2,1)} %get-tuple-element.163.c_ref, bf16[1500,512]{1,0:T(8,128)(2,1)} %x_ref.7, ...), custom_call_target="tpu_custom_call" | custom-call | flops 38000001024 | bytes 1048576 | tf_op jit(solution)/shard_map/middle/pallas_call | solution.py:835
  103.4 0.1 collective-permute-start.15
  103.5 14.5 %attend_backward.3 = (bf16[1536,512]{1,0:T(8,128)(2,1)S(1)}, bf16[1536,512]{1,0:T(8,128)(2,1)S(1)}, bf16[1536,512]{1,0:T(8,128)(2,1)S(1)}, bf16[2,3,512,256]{3,2,1,0:T(8,128)(2,1)S(1)}, f32[8,512]{1,0:T(8,128)S(1)}) custom-call(bf16[1536,512]{1,0:T(8,128)(2,1)S(1)} %get-tuple-element.167.q_ref, bf16[1536,512]{1,0:T(8,128)(2,1)S(1)} %get-tuple-element.168.k_ref, ...), custom_call_target="tpu_custom_call" | custom-call | flops 14000000000 | bytes 1048576 | tf_op jit(solution)/shard_map/attend_backward/pallas_call | solution.py:675
  118.0 0.6 spread.4
  118.6 1.4 collective-permute-start.16
  120.0 0.5 collective-permute-start.17
  120.5 1.7 collective-permute-start.18
  122.2 26.6 %attend_backward.4 = (bf16[1536,512]{1,0:T(8,128)(2,1)S(1)}, bf16[1536,512]{1,0:T(8,128)(2,1)S(1)}, bf16[1536,512]{1,0:T(8,128)(2,1)S(1)}, bf16[2,3,512,256]{3,2,1,0:T(8,128)(2,1)S(1)}, f32[8,512]{1,0:T(8,128)S(1)}) custom-call(bf16[1536,512]{1,0:T(8,128)(2,1)S(1)} %get-tuple-element.167., ...), custom_call_target="tpu_custom_call", output_to_operand_aliasing={{0}: (11, {}), {1}: (12, {}), {2}: (13, {}), {3}: (14, {})} | custom-call | flops 28000000000 | bytes 1048576 | tf_op jit(solution)/shard_map/attend_backward/pallas_call | solution.py:675
  148.8 0.1 slice_bitcast_fusion
  148.9 0.3 spread.5
  149.2 1.4 collective-permute-start.22
  150.6 0.3 collective-permute-start.19
  150.8 0.1 collective-permute-start.20
  150.9 4.0 %collective-permute-start.21 = (bf16[320,256]{1,0:T(8,128)(2,1)S(1)}, bf16[320,256]{1,0:T(8,128)(2,1)S(1)}, u32[]{:S(2)}, u32[]{:S(2)}) collective-permute-start(bf16[320,256]{1,0:T(8,128)(2,1)S(1)} %get-tuple-element.211), channel_id=1, source_target_pairs={{0,24},{1,25},{2,26},{3,27},{4,28},{5,29},{6,30},{7,31},{8,16},{9,... | collective-permute-start | bytes 491528 | tf_op jit(solution)/shard_map/ppermute | solution.py:929
  154.9 14.3 %attend_backward.5 = (bf16[1536,512]{1,0:T(8,128)(2,1)S(1)}, bf16[1536,512]{1,0:T(8,128)(2,1)S(1)}, bf16[1536,512]{1,0:T(8,128)(2,1)S(1)}, bf16[2,3,512,256]{3,2,1,0:T(8,128)(2,1)S(1)}, f32[8,512]{1,0:T(8,128)S(1)}) custom-call(bf16[1536,512]{1,0:T(8,128)(2,1)S(1)} %get-tuple-element.167., ...), custom_call_target="tpu_custom_call", output_to_operand_aliasing={{0}: (11, {}), {1}: (12, {}), {2}: (13, {}), {3}: (14, {})} | custom-call | flops 14000000000 | bytes 1048576 | tf_op jit(solution)/shard_map/attend_backward/pallas_call | solution.py:675
  169.3 0.3 gather_grads.1
  169.7 0.1 collective-permute-start.23
  169.7 1.7 collective-permute-done.23.refs_0_
  171.5 0.1 spread.6
  171.6 0.1 collective-permute-start.24
  171.6 0.6 collective-permute-start.25
  172.2 2.9 %collective-permute-start.26 = (bf16[208,256]{1,0:T(8,128)(2,1)S(1)}, bf16[208,256]{1,0:T(8,128)(2,1)S(1)}, u32[]{:S(2)}, u32[]{:S(2)}) collective-permute-start(bf16[208,256]{1,0:T(8,128)(2,1)S(1)} %get-tuple-element.223), channel_id=1, source_target_pairs={{0,12},{1,13},{2,14},{3,15},{4,8},{5,9},{6,10},{7,11},{8,4},{9,5},... | collective-permute-start | bytes 319496 | tf_op jit(solution)/shard_map/ppermute | solution.py:929
  175.1 3.7 %input_grads.2.refs_0_ = bf16[1500,512]{1,0:T(8,128)(2,1)} custom-call(bf16[1500,512]{1,0:T(8,128)(2,1)S(1)} %copy-done.3, f32[1536,512]{1,0:T(8,128)S(1)} %copy-done.1, f32[16,512]{1,0:T(8,128)S(1)} %copy-done.5, bf16[3,512,512]{2,1,0:T(8,128)(2,1)S(1)} %copy-done, bf16[1536,512]{1,0:T(8,128)(2,1)S(1)} %get-tuple-element.225.dq_ref, ...), custom_call_target="tpu_custom_call" | custom-call | flops 4000000000 | bytes 1048576 | tf_op jit(solution)/shard_map/input_grads/pallas_call | solution.py:1063
  178.8 0.2 collective-permute-done.25.refs_1_
  179.0 0.1 spread.7
  179.1 0.3 collective-permute-start.27
  179.3 1.2 collective-permute-start.28
  180.5 3.0 %collective-permute-start.29 = (bf16[16,256]{1,0:T(8,128)(2,1)S(1)}, bf16[16,256]{1,0:T(8,128)(2,1)S(1)}, u32[]{:S(2)}, u32[]{:S(2)}) collective-permute-start(bf16[16,256]{1,0:T(8,128)(2,1)S(1)} %get-tuple-element.233), channel_id=1, source_target_pairs={{0,17},{1,16},{2,19},{3,18},{4,21},{5,20},{6,23},{7,22},{8,25},{9,... | collective-permute-start | bytes 24584 | tf_op jit(solution)/shard_map/ppermute | solution.py:929
  183.5 2.2 %input_grads.3 = bf16[1500,512]{1,0:T(8,128)(2,1)} custom-call(bf16[1500,512]{1,0:T(8,128)(2,1)S(1)} %copy-done.3, f32[1536,512]{1,0:T(8,128)S(1)} %copy-done.1, f32[16,512]{1,0:T(8,128)S(1)} %copy-done.5, bf16[3,512,512]{2,1,0:T(8,128)(2,1)S(1)} %copy-done, bf16[1536,512]{1,0:T(8,128)(2,1)S(1)} %get-tuple-element.225.dq_ref, ...), custom_call_target="tpu_custom_call", output_to_operand_aliasing={{}: (7, {})} | custom-call | flops 2000000000 | bytes 1048576 | tf_op jit(solution)/shard_map/input_grads/pallas_call | solution.py:1063
  185.7 0.3 collective-permute-done.29.refs_5_
  186.0 0.8 finish.1
  (37 shorter events, 0.2 us)
Async XLA Ops:
  0.7 6.0 %copy-start.2 = (bf16[1500,512]{1,0:T(8,128)(2,1)S(1)}, bf16[1500,512]{1,0:T(8,128)(2,1)}, u32[]{:S(2)}) copy-start(bf16[1500,512]{1,0:T(8,128)(2,1)} %x_ref.7) | copy-start | bytes 4608004
  2.7 7.0 %collective-permute-start = (bf16[1,96,256]{2,1,0:T(8,128)(2,1)}, bf16[1,96,256]{2,1,0:T(8,128)(2,1)S(1)}, u32[]{:S(2)}, u32[]{:S(2)}) collective-permute-start(bf16[1,96,256]{2,1,0:T(8,128)(2,1)} %get-tuple-element.139), channel_id=1, source_target_pairs={{0,16},{1,17},{2,18},{3,19},{4,20},{5,21},{6,22},{7,23},{8,24},{9,... | collective-permute-start | bytes 147464 | tf_op jit(solution)/shard_map/ppermute | solution.py:929
  6.7 0.8 copy-start.4
  7.5 2.1 %copy-start.6 = (bf16[1,96,256]{2,1,0:T(8,128)(2,1)S(1)}, bf16[1,96,256]{2,1,0:T(8,128)(2,1)}, u32[]{:S(2)}) copy-start(bf16[1,96,256]{2,1,0:T(8,128)(2,1)} %get-tuple-element.139) | copy-start | bytes 147460
  7.5 3.8 %copy-start.7 = (bf16[288,256]{1,0:T(8,128)(2,1)S(1)}, bf16[288,256]{1,0:T(8,128)(2,1)}, u32[]{:S(2)}) copy-start(bf16[288,256]{1,0:T(8,128)(2,1)} %get-tuple-element.144) | copy-start | bytes 442372
  9.6 22.6 %copy-start.5 = (f32[16,512]{1,0:T(8,128)S(1)}, f32[16,512]{1,0:T(8,128)}, u32[]{:S(2)}) copy-start(f32[16,512]{1,0:T(8,128)} %get-tuple-element.140.table_ref) | copy-start | bytes 98308
  9.7 4.7 %collective-permute-start.1 = (bf16[2,96,256]{2,1,0:T(8,128)(2,1)S(1)}, bf16[2,96,256]{2,1,0:T(8,128)(2,1)S(1)}, u32[]{:S(2)}, u32[]{:S(2)}) collective-permute-start(bf16[2,96,256]{2,1,0:T(8,128)(2,1)S(1)} %get-tuple-element.261), channel_id=1, source_target_pairs={{0,8},{1,9},{2,10},{3,11},{4,12},{5,13},{6,14},{7,15},{8,0},{9,1},... | collective-permute-start | bytes 294920 | tf_op jit(solution)/shard_map/ppermute | solution.py:929
  11.3 9.0 %collective-permute-start.4 = (bf16[1,288,256]{2,1,0:T(8,128)(2,1)S(1)}, bf16[1,288,256]{2,1,0:T(8,128)(2,1)S(1)}, u32[]{:S(2)}, u32[]{:S(2)}) collective-permute-start(bf16[1,288,256]{2,1,0:T(8,128)(2,1)S(1)} %bitcast.25), channel_id=1, source_target_pairs={{0,16},{1,17},{2,18},{3,19},{4,20},{5,21},{6,22},{7,23},{8,24},{9,... | collective-permute-start | bytes 442376 | tf_op jit(solution)/shard_map/ppermute | solution.py:929
  14.4 6.0 %collective-permute-start.2 = (bf16[4,96,256]{2,1,0:T(8,128)(2,1)S(1)}, bf16[4,96,256]{2,1,0:T(8,128)(2,1)S(1)}, u32[]{:S(2)}, u32[]{:S(2)}) collective-permute-start(bf16[4,96,256]{2,1,0:T(8,128)(2,1)S(1)} %pad_maximum_fusion.2), channel_id=1, source_target_pairs={{0,4},{1,5},{2,6},{3,7},{4,0},{5,1},{6,2},{7,3},{8,12},{9,13},{10,... | collective-permute-start | bytes 589832 | tf_op jit(solution)/shard_map/ppermute | solution.py:929
  20.4 8.8 %collective-permute-start.5 = (bf16[2,288,256]{2,1,0:T(8,128)(2,1)S(1)}, bf16[2,288,256]{2,1,0:T(8,128)(2,1)S(1)}, u32[]{:S(2)}, u32[]{:S(2)}) collective-permute-start(bf16[2,288,256]{2,1,0:T(8,128)(2,1)S(1)} %pad_maximum_fusion.1), channel_id=1, source_target_pairs={{0,8},{1,9},{2,10},{3,11},{4,12},{5,13},{6,14},{7,15},{8,0},{9,1},... | collective-permute-start | bytes 884744 | tf_op jit(solution)/shard_map/ppermute | solution.py:929
  20.5 8.7 %collective-permute-start.6 = (bf16[8,96,256]{2,1,0:T(8,128)(2,1)S(1)}, bf16[8,96,256]{2,1,0:T(8,128)(2,1)S(1)}, u32[]{:S(2)}, u32[]{:S(2)}) collective-permute-start(bf16[8,96,256]{2,1,0:T(8,128)(2,1)S(1)} %constant_dynamic-update-slice_fusion.2.near_ref), channel_id=1, source_target_pairs={{0,2},{1,3},{2,0},{3,1},{4,6},{5,7},{6,4},{7,5},{8,10},{9,11},{10,... | collective-permute-start | bytes 1179656 | tf_op jit(solution)/shard_map/ppermute | solution.py:929
  20.5 28.7 %collective-permute-start.3 = (bf16[8,96,256]{2,1,0:T(8,128)(2,1)S(1)}, bf16[8,96,256]{2,1,0:T(8,128)(2,1)S(1)}, u32[]{:S(2)}, u32[]{:S(2)}) collective-permute-start(bf16[8,96,256]{2,1,0:T(8,128)(2,1)S(1)} %constant_dynamic-update-slice_fusion.2.near_ref), channel_id=1, source_target_pairs={{0,1},{1,0},{2,3},{3,2},{4,5},{5,4},{6,7},{7,6},{8,9},{9,8},{10,11... | collective-permute-start | bytes 1179656 | tf_op jit(solution)/shard_map/ppermute | solution.py:929
  29.2 20.1 %collective-permute-start.7 = (bf16[4,288,256]{2,1,0:T(8,128)(2,1)S(1)}, bf16[4,288,256]{2,1,0:T(8,128)(2,1)S(1)}, u32[]{:S(2)}, u32[]{:S(2)}) collective-permute-start(bf16[4,288,256]{2,1,0:T(8,128)(2,1)S(1)} %pad_maximum_fusion.refs_0_), channel_id=1, source_target_pairs={{0,4},{1,5},{2,6},{3,7},{4,0},{5,1},{6,2},{7,3},{8,12},{9,13},{10,... | collective-permute-start | bytes 1769480 | tf_op jit(solution)/shard_map/ppermute | solution.py:929
  30.8 18.5 %collective-permute-start.8 = (bf16[4,288,256]{2,1,0:T(8,128)(2,1)S(1)}, bf16[4,288,256]{2,1,0:T(8,128)(2,1)S(1)}, u32[]{:S(2)}, u32[]{:S(2)}) collective-permute-start(bf16[4,288,256]{2,1,0:T(8,128)(2,1)S(1)} %pad_maximum_fusion.refs_0_), channel_id=1, source_target_pairs={{0,1},{1,0},{2,3},{3,2},{4,5},{5,4},{6,7},{7,6},{8,9},{9,8},{10,11... | collective-permute-start | bytes 1769480 | tf_op jit(solution)/shard_map/ppermute | solution.py:929
  49.3 1.8 collective-permute-start.10
  49.3 19.0 %collective-permute-start.11 = (bf16[4,288,256]{2,1,0:T(8,128)(2,1)S(1)}, bf16[4,288,256]{2,1,0:T(8,128)(2,1)S(1)}, u32[]{:S(2)}, u32[]{:S(2)}) collective-permute-start(bf16[4,288,256]{2,1,0:T(8,128)(2,1)S(1)} %pad_maximum_fusion.refs_0_), channel_id=1, source_target_pairs={{0,2},{1,3},{2,0},{3,1},{4,6},{5,7},{6,4},{7,5},{8,10},{9,11},{10,... | collective-permute-start | bytes 1769480 | tf_op jit(solution)/shard_map/ppermute | solution.py:929
  49.8 18.3 %collective-permute-start.9 = (bf16[4,288,256]{2,1,0:T(8,128)(2,1)S(1)}, bf16[4,288,256]{2,1,0:T(8,128)(2,1)S(1)}, u32[]{:S(2)}, u32[]{:S(2)}) collective-permute-start(bf16[4,288,256]{2,1,0:T(8,128)(2,1)S(1)} %collective-permute-done.7.refs_1_), channel_id=1, source_target_pairs={{0,1},{1,0},{2,3},{3,2},{4,5},{5,4},{6,7},{7,6},{8,9},{9,8},{10,11... | collective-permute-start | bytes 1769480 | tf_op jit(solution)/shard_map/ppermute | solution.py:929
  50.4 17.9 %collective-permute-start.12 = (bf16[4,288,256]{2,1,0:T(8,128)(2,1)S(1)}, bf16[4,288,256]{2,1,0:T(8,128)(2,1)S(1)}, u32[]{:S(2)}, u32[]{:S(2)}) collective-permute-start(bf16[4,288,256]{2,1,0:T(8,128)(2,1)S(1)} %collective-permute-done.7.refs_1_), channel_id=1, source_target_pairs={{0,2},{1,3},{2,0},{3,1},{4,6},{5,7},{6,4},{7,5},{8,10},{9,11},{10,... | collective-permute-start | bytes 1769480 | tf_op jit(solution)/shard_map/ppermute | solution.py:929
  50.4 17.9 %collective-permute-start.13 = (bf16[4,288,256]{2,1,0:T(8,128)(2,1)S(1)}, bf16[4,288,256]{2,1,0:T(8,128)(2,1)S(1)}, u32[]{:S(2)}, u32[]{:S(2)}) collective-permute-start(bf16[4,288,256]{2,1,0:T(8,128)(2,1)S(1)} %collective-permute-done.8.refs_2_), channel_id=1, source_target_pairs={{0,2},{1,3},{2,0},{3,1},{4,6},{5,7},{6,4},{7,5},{8,10},{9,11},{10,... | collective-permute-start | bytes 1769480 | tf_op jit(solution)/shard_map/ppermute | solution.py:929
  68.1 2.1 %collective-permute-start.14 = (bf16[4,288,256]{2,1,0:T(8,128)(2,1)S(1)}, bf16[4,288,256]{2,1,0:T(8,128)(2,1)S(1)}, u32[]{:S(2)}, u32[]{:S(2)}) collective-permute-start(bf16[4,288,256]{2,1,0:T(8,128)(2,1)S(1)} %collective-permute-done.9.refs_3_), channel_id=1, source_target_pairs={{0,2},{1,3},{2,0},{3,1},{4,6},{5,7},{6,4},{7,5},{8,10},{9,11},{10,... | collective-permute-start | bytes 1769480 | tf_op jit(solution)/shard_map/ppermute | solution.py:929
  103.4 14.6 %collective-permute-start.15 = (bf16[4640,256]{1,0:T(8,128)(2,1)S(1)}, bf16[4640,256]{1,0:T(8,128)(2,1)S(1)}, u32[]{:S(2)}, u32[]{:S(2)}) collective-permute-start(bf16[4640,256]{1,0:T(8,128)(2,1)S(1)} %get-tuple-element.175), channel_id=1, source_target_pairs={{0,2},{1,3},{2,0},{3,1},{4,6},{5,7},{6,4},{7,5},{8,10},{9,11},{10,... | collective-permute-start | bytes 7127048 | tf_op jit(solution)/shard_map/ppermute | solution.py:929
  118.6 30.3 %collective-permute-start.16 = (bf16[1184,256]{1,0:T(8,128)(2,1)S(1)}, bf16[1184,256]{1,0:T(8,128)(2,1)S(1)}, u32[]{:S(2)}, u32[]{:S(2)}) collective-permute-start(bf16[1184,256]{1,0:T(8,128)(2,1)S(1)} %get-tuple-element.184), channel_id=1, source_target_pairs={{0,1},{1,0},{2,3},{3,2},{4,5},{5,4},{6,7},{7,6},{8,9},{9,8},{10,11... | collective-permute-start | bytes 1818632 | tf_op jit(solution)/shard_map/ppermute | solution.py:929
  120.0 28.9 %collective-permute-start.17 = (bf16[1184,256]{1,0:T(8,128)(2,1)S(1)}, bf16[1184,256]{1,0:T(8,128)(2,1)S(1)}, u32[]{:S(2)}, u32[]{:S(2)}) collective-permute-start(bf16[1184,256]{1,0:T(8,128)(2,1)S(1)} %get-tuple-element.185), channel_id=1, source_target_pairs={{0,4},{1,5},{2,6},{3,7},{4,0},{5,1},{6,2},{7,3},{8,12},{9,13},{10,... | collective-permute-start | bytes 1818632 | tf_op jit(solution)/shard_map/ppermute | solution.py:929
  120.5 28.4 %collective-permute-start.18 = (bf16[1184,256]{1,0:T(8,128)(2,1)S(1)}, bf16[1184,256]{1,0:T(8,128)(2,1)S(1)}, u32[]{:S(2)}, u32[]{:S(2)}) collective-permute-start(bf16[1184,256]{1,0:T(8,128)(2,1)S(1)} %get-tuple-element.186), channel_id=1, source_target_pairs={{0,5},{1,4},{2,7},{3,6},{4,1},{5,0},{6,3},{7,2},{8,13},{9,12},{10,... | collective-permute-start | bytes 1818632 | tf_op jit(solution)/shard_map/ppermute | solution.py:929
  149.2 20.1 %collective-permute-start.22 = (bf16[3,512,256]{2,1,0:T(8,128)(2,1)S(1)}, bf16[3,512,256]{2,1,0:T(8,128)(2,1)S(1)}, u32[]{:S(2)}, u32[]{:S(2)}) collective-permute-start(bf16[3,512,256]{2,1,0:T(8,128)(2,1)S(1)} %slice_bitcast_fusion), channel_id=1, source_target_pairs={{0,1},{1,0},{2,3},{3,2},{4,5},{5,4},{6,7},{7,6},{8,9},{9,8},{10,11... | collective-permute-start | bytes 2359304 | tf_op jit(solution)/shard_map/ppermute | solution.py:929
  150.6 18.7 %collective-permute-start.19 = (bf16[320,256]{1,0:T(8,128)(2,1)S(1)}, bf16[320,256]{1,0:T(8,128)(2,1)S(1)}, u32[]{:S(2)}, u32[]{:S(2)}) collective-permute-start(bf16[320,256]{1,0:T(8,128)(2,1)S(1)} %get-tuple-element.209), channel_id=1, source_target_pairs={{0,8},{1,9},{2,10},{3,11},{4,12},{5,13},{6,14},{7,15},{8,0},{9,1},... | collective-permute-start | bytes 491528 | tf_op jit(solution)/shard_map/ppermute | solution.py:929
  150.8 18.5 %collective-permute-start.20 = (bf16[320,256]{1,0:T(8,128)(2,1)S(1)}, bf16[320,256]{1,0:T(8,128)(2,1)S(1)}, u32[]{:S(2)}, u32[]{:S(2)}) collective-permute-start(bf16[320,256]{1,0:T(8,128)(2,1)S(1)} %get-tuple-element.210), channel_id=1, source_target_pairs={{0,16},{1,17},{2,18},{3,19},{4,20},{5,21},{6,22},{7,23},{8,24},{9,... | collective-permute-start | bytes 491528 | tf_op jit(solution)/shard_map/ppermute | solution.py:929
  150.9 18.4 %collective-permute-start.21 = (bf16[320,256]{1,0:T(8,128)(2,1)S(1)}, bf16[320,256]{1,0:T(8,128)(2,1)S(1)}, u32[]{:S(2)}, u32[]{:S(2)}) collective-permute-start(bf16[320,256]{1,0:T(8,128)(2,1)S(1)} %get-tuple-element.211), channel_id=1, source_target_pairs={{0,24},{1,25},{2,26},{3,27},{4,28},{5,29},{6,30},{7,31},{8,16},{9,... | collective-permute-start | bytes 491528 | tf_op jit(solution)/shard_map/ppermute | solution.py:929
  169.7 1.8 collective-permute-start.23
  171.5 3.7 %copy-start = (bf16[3,512,512]{2,1,0:T(8,128)(2,1)S(1)}, bf16[3,512,512]{2,1,0:T(8,128)(2,1)}, u32[]{:S(2)}) copy-start(bf16[3,512,512]{2,1,0:T(8,128)(2,1)} %get-tuple-element.188.w_ref) | copy-start | bytes 4718596
  171.5 3.7 %copy-start.1 = (f32[1536,512]{1,0:T(8,128)S(1)}, f32[1536,512]{1,0:T(8,128)}, u32[]{:S(2)}) copy-start(f32[1536,512]{1,0:T(8,128)} %get-tuple-element.224.gh_ref) | copy-start | bytes 9437188
  171.5 3.7 %copy-start.3 = (bf16[1500,512]{1,0:T(8,128)(2,1)S(1)}, bf16[1500,512]{1,0:T(8,128)(2,1)}, u32[]{:S(2)}) copy-start(bf16[1500,512]{1,0:T(8,128)(2,1)} %x_ref.7) | copy-start | bytes 4608004
  171.6 7.2 %collective-permute-start.24 = (bf16[208,256]{1,0:T(8,128)(2,1)S(1)}, bf16[208,256]{1,0:T(8,128)(2,1)S(1)}, u32[]{:S(2)}, u32[]{:S(2)}) collective-permute-start(bf16[208,256]{1,0:T(8,128)(2,1)S(1)} %get-tuple-element.221), channel_id=1, source_target_pairs={{0,8},{1,9},{2,10},{3,11},{4,12},{5,13},{6,14},{7,15},{8,0},{9,1},... | collective-permute-start | bytes 319496 | tf_op jit(solution)/shard_map/ppermute | solution.py:929
  171.6 7.4 %collective-permute-start.25 = (bf16[208,256]{1,0:T(8,128)(2,1)S(1)}, bf16[208,256]{1,0:T(8,128)(2,1)S(1)}, u32[]{:S(2)}, u32[]{:S(2)}) collective-permute-start(bf16[208,256]{1,0:T(8,128)(2,1)S(1)} %get-tuple-element.222), channel_id=1, source_target_pairs={{0,4},{1,5},{2,6},{3,7},{4,0},{5,1},{6,2},{7,3},{8,12},{9,13},{10,... | collective-permute-start | bytes 319496 | tf_op jit(solution)/shard_map/ppermute | solution.py:929
  172.2 6.8 %collective-permute-start.26 = (bf16[208,256]{1,0:T(8,128)(2,1)S(1)}, bf16[208,256]{1,0:T(8,128)(2,1)S(1)}, u32[]{:S(2)}, u32[]{:S(2)}) collective-permute-start(bf16[208,256]{1,0:T(8,128)(2,1)S(1)} %get-tuple-element.223), channel_id=1, source_target_pairs={{0,12},{1,13},{2,14},{3,15},{4,8},{5,9},{6,10},{7,11},{8,4},{9,5},... | collective-permute-start | bytes 319496 | tf_op jit(solution)/shard_map/ppermute | solution.py:929
  179.1 6.9 %collective-permute-start.27 = (bf16[112,256]{1,0:T(8,128)(2,1)S(1)}, bf16[112,256]{1,0:T(8,128)(2,1)S(1)}, u32[]{:S(2)}, u32[]{:S(2)}) collective-permute-start(bf16[112,256]{1,0:T(8,128)(2,1)S(1)} %get-tuple-element.231), channel_id=1, source_target_pairs={{0,16},{1,17},{2,18},{3,19},{4,20},{5,21},{6,22},{7,23},{8,24},{9,... | collective-permute-start | bytes 172040 | tf_op jit(solution)/shard_map/ppermute | solution.py:929
  179.3 6.3 %collective-permute-start.28 = (bf16[16,256]{1,0:T(8,128)(2,1)S(1)}, bf16[16,256]{1,0:T(8,128)(2,1)S(1)}, u32[]{:S(2)}, u32[]{:S(2)}) collective-permute-start(bf16[16,256]{1,0:T(8,128)(2,1)S(1)} %get-tuple-element.232), channel_id=1, source_target_pairs={{0,1},{1,0},{2,3},{3,2},{4,5},{5,4},{6,7},{7,6},{8,9},{9,8},{10,11... | collective-permute-start | bytes 24584 | tf_op jit(solution)/shard_map/ppermute | solution.py:929
  180.5 5.4 %collective-permute-start.29 = (bf16[16,256]{1,0:T(8,128)(2,1)S(1)}, bf16[16,256]{1,0:T(8,128)(2,1)S(1)}, u32[]{:S(2)}, u32[]{:S(2)}) collective-permute-start(bf16[16,256]{1,0:T(8,128)(2,1)S(1)} %get-tuple-element.233), channel_id=1, source_target_pairs={{0,17},{1,16},{2,19},{3,18},{4,21},{5,20},{6,23},{7,22},{8,25},{9,... | collective-permute-start | bytes 24584 | tf_op jit(solution)/shard_map/ppermute | solution.py:929
